TPU v7x, 256 devices: a whole 4x4x8 slice. The times are simulated.
256 devices in a mesh: row: 8 (over z), col: 8 (over x, core), sub: 4 (over y).
Axes of the slice: x: 4, y: 4, z: 8, core: 2. Of those that a mesh axis runs over, the one named last changes fastest.
Arguments:
- front_entries: float32 [8192, 8192], P('row', ('col', 'sub')), may hold values from -1 to 4, as said below
- child_blocks: float32 [4, 2048, 2048], P('sub', 'row', 'col'), may hold values from -1 to 2, as said below
- child_map: int32 [4, 16], P('sub'), may hold values from 0 to 63, as said below
Outputs:
- factored: float32 [8192, 8192], P('row', ('col', 'sub'))
Inputs may be any that keep to these rules, and one draw needn't show every extreme that they name: Each row of child_map lists 16 different parent blocks in increasing order and ends with block 63. In natural order front_entries is a symmetric matrix, and the assembled front is positive definite. `child_blocks`: in natural order each child's contribution block is a symmetric matrix.
All inputs are finite; a program needn't handle non-finite values.
Results may differ from a plain program's by a relative error of at most 0.00005.
Values sent between devices are 32-bit elements; how exact they have to be, the bound alone decides.
A program may use at most 128 MiB of HBM per device.

v0:
```python
import jax
import jax.numpy as jnp
from jax import lax
from jax.sharding import PartitionSpec as P

BLK = 128
NPIV = 6


highest = lax.Precision.HIGHEST


def broadcast(value, axis, source):
    kept = jnp.where(lax.axis_index(axis) == source, value, 0).astype(value.dtype)
    return lax.psum(kept, axis)


def lookup(index_table, wanted):
    positions = jnp.arange(index_table.shape[0], dtype=jnp.int32)
    return jnp.sum(jnp.where(wanted[..., None] == positions, index_table, 0), axis=-1)


def body(front_entries, child_blocks, child_map):
    row_count = lax.axis_size("row")
    col_count = lax.axis_size("col")
    sub_count = lax.axis_size("sub")
    row_index = lax.axis_index("row")
    col_index = lax.axis_index("col")
    sub_index = lax.axis_index("sub")
    child_tile = child_blocks[0]
    mapping = child_map[0]
    local_rows = front_entries.shape[0]
    row_blocks = local_rows // BLK
    slot_count = front_entries.shape[1] // BLK
    col_blocks = slot_count * sub_count
    child_rows = child_tile.shape[0] // BLK
    child_cols = child_tile.shape[1] // BLK
    zero_carry = jnp.zeros((row_blocks, BLK, col_blocks, BLK), jnp.float32)
    incoming = lax.all_gather(child_tile[None], ("row", "col"), axis=0, tiled=True)
    piece_count = incoming.shape[0]
    source = jnp.arange(piece_count, dtype=jnp.int32)
    source_row = source // col_count
    source_col = source % col_count
    row_parent = lookup(
        mapping, jnp.arange(child_rows, dtype=jnp.int32)[None, :] * row_count + source_row[:, None]
    )
    col_parent = lookup(
        mapping, jnp.arange(child_cols, dtype=jnp.int32)[None, :] * col_count + source_col[:, None]
    )
    row_target = jnp.where(row_parent % row_count == row_index, row_parent // row_count, row_blocks)
    col_target = jnp.where(col_parent % col_count == col_index, col_parent // col_count, col_blocks)
    tile_stack = incoming.reshape(piece_count, child_rows, BLK, child_cols, BLK).transpose(
        0, 1, 3, 2, 4
    )
    spread_sum = zero_carry.at[row_target[:, :, None], :, col_target[:, None, :], :].add(
        tile_stack, mode="drop"
    )
    spread_sum = spread_sum.reshape(local_rows, col_blocks * BLK)
    summed = lax.psum_scatter(spread_sum, "sub", scatter_dimension=1, tiled=True)
    matrix = front_entries + summed
    row_global = jnp.repeat(jnp.arange(row_blocks, dtype=jnp.int32) * row_count + row_index, BLK)
    col_global = jnp.repeat(
        (sub_index * slot_count + jnp.arange(slot_count, dtype=jnp.int32)) * col_count + col_index,
        BLK,
    )
    for pivot_step in range(NPIV):
        sources_col_slot = pivot_step // col_count % slot_count
        sources_pivot_block = pivot_step // row_count
        col_source = matrix[:, sources_col_slot * BLK : (sources_col_slot + 1) * BLK]
        row_source = matrix[sources_pivot_block * BLK : (sources_pivot_block + 1) * BLK, :]
        root_group = pivot_step % col_count * sub_count + pivot_step // col_count // slot_count
        share_col_panel = broadcast(col_source, ("col", "sub"), root_group)
        pivot_block = pivot_step // row_count
        share_diagonal = share_col_panel[pivot_block * BLK : (pivot_block + 1) * BLK, :]
        share_pivot_row_panel, share_diagonal = (
            broadcast(row_source, "row", pivot_step % row_count),
            broadcast(share_diagonal, "row", pivot_step % row_count),
        )
        pivot_factor = jnp.linalg.cholesky(share_diagonal)
        lower_rows = jax.scipy.linalg.solve_triangular(
            pivot_factor, share_col_panel.T, lower=True
        ).T
        upper_rows = jax.scipy.linalg.solve_triangular(
            pivot_factor, share_pivot_row_panel, lower=True
        )
        left_factor = jnp.where(row_global[:, None] > pivot_step, lower_rows, 0.0)
        right_factor = jnp.where(col_global[None, :] > pivot_step, upper_rows, 0.0)
        factor_column = jnp.where(row_global[:, None] >= pivot_step, lower_rows, 0.0)
        left_factor, right_factor, column = (left_factor, right_factor, factor_column)
        matrix = matrix - jnp.dot(left_factor, right_factor, precision=highest)
        col_slot = pivot_step // col_count % slot_count
        is_owner = (col_index == pivot_step % col_count) & (
            sub_index == pivot_step // col_count // slot_count
        )
        existing = matrix[:, col_slot * BLK : (col_slot + 1) * BLK]
        matrix = matrix.at[:, col_slot * BLK : (col_slot + 1) * BLK].set(
            jnp.where(is_owner, column, existing)
        )
    upper_right = (row_global[:, None] < NPIV) & (col_global[None, :] >= NPIV)
    return jnp.where(upper_right, 0.0, matrix)


def solution(mesh):
    placed = (P("row", ("col", "sub")), P("sub", "row", "col"), P("sub", None))
    return jax.shard_map(
        body, mesh=mesh, in_specs=placed, out_specs=P("row", ("col", "sub")), check_vma=False
    )
```

profile of v0, /device:TPU:2, one launch (start us, length us, event | category | flops | bytes accessed | tf_op | source)
XLA Modules:
  0.0 1575.8 jit_solution(9138514772814132844)
XLA Ops:
  9.0 102.0 %all-gather.2.cloned.1.call-done = f32[64,256,256]{2,1,0:T(8,128)} async-done(((f32[1,256,256]{2,1,0:T(8,128)}), f32[64,256,256]{2,1,0:T(8,128)}) %all-gather.2.cloned.1.call-update) | async-done | bytes 16777232 | tf_op jit(solution)/shard_map/all_gather | solution.py:39
  111.0 20.8 %reshape.466 = f32[64,2,128,2,128]{4,3,2,1,0:T(2,128)} reshape(f32[64,256,256]{2,1,0:T(8,128)} %all-gather.2.cloned.1.call-done) | data formatting | bytes 33554432 | tf_op jit(solution)/shard_map/reshape | solution.py:52
  131.8 12.6 copy.62
  146.9 50.2 %scatter_fusion = f32[8,128,8,128]{3,1,2,0:T(8,128)} fusion(f32[8,128,8,128]{3,1,2,0:T(8,128)} %broadcast_in_dim.231, s32[256]{0:T(256)S(1)} %reshape.468, f32[256,128,128]{2,1,0:T(8,128)} %bitcast.192), kind=kCustom, calls=%fused_computation | custom fusion | flops 4194304 | bytes 50333696 | tf_op jit(solution)/shard_map/scatter-add | solution.py:55
  209.1 47.0 %reduce-scatter.2.cloned.1.call-done = f32[1024,256]{0,1:T(8,128)} async-done(((f32[1024,1024]{0,1:T(8,128)}), f32[1024,256]{0,1:T(8,128)}) %reduce-scatter.2.cloned.1.call-update) | async-done | bytes 1048592 | tf_op jit(solution)/shard_map/reduce_scatter | solution.py:59
  259.7 113.2 %all-reduce.19.cloned.1.call-done = f32[1024,128]{0,1:T(8,128)} async-done(((f32[1024,128]{0,1:T(8,128)}), f32[1024,128]{0,1:T(8,128)}) %all-reduce.19.cloned.1.call-update) | async-done | bytes 524304 | tf_op jit(solution)/shard_map/psum | solution.py:15
  375.0 73.2 %all-reduce.41.cloned.1.call-done = (f32[128,256]{0,1:T(8,128)}, f32[128,128]{0,1:T(8,128)}) async-done(((f32[128,256]{0,1:T(8,128)}, f32[128,128]{0,1:T(8,128)}), (f32[128,256]{0,1:T(8,128)}, f32[128,128]{0,1:T(8,128)})) %all-reduce.41.cloned.1.call-update) | async-done | bytes 196624 | tf_op jit(solution)/shard_map/psum | solution.py:15
  450.0 11.7 cholesky.104
  479.2 111.6 %all-reduce.21.cloned.1.call-done = f32[1024,128]{0,1:T(8,128)} async-done(((f32[1024,128]{0,1:T(8,128)}), f32[1024,128]{0,1:T(8,128)}) %all-reduce.21.cloned.1.call-update) | async-done | bytes 524304 | tf_op jit(solution)/shard_map/psum | solution.py:15
  592.6 73.6 %all-reduce.39.cloned.1.call-done = (f32[128,256]{0,1:T(8,128)}, f32[128,128]{0,1:T(8,128)}) async-done(((f32[128,256]{0,1:T(8,128)}, f32[128,128]{0,1:T(8,128)}), (f32[128,256]{0,1:T(8,128)}, f32[128,128]{0,1:T(8,128)})) %all-reduce.39.cloned.1.call-update) | async-done | bytes 196624 | tf_op jit(solution)/shard_map/psum | solution.py:15
  668.0 11.7 cholesky.115
  697.1 111.7 %all-reduce.23.cloned.1.call-done = f32[1024,128]{0,1:T(8,128)} async-done(((f32[1024,128]{0,1:T(8,128)}), f32[1024,128]{0,1:T(8,128)}) %all-reduce.23.cloned.1.call-update) | async-done | bytes 524304 | tf_op jit(solution)/shard_map/psum | solution.py:15
  810.6 73.7 %all-reduce.37.cloned.1.call-done = (f32[128,256]{0,1:T(8,128)}, f32[128,128]{0,1:T(8,128)}) async-done(((f32[128,256]{0,1:T(8,128)}, f32[128,128]{0,1:T(8,128)}), (f32[128,256]{0,1:T(8,128)}, f32[128,128]{0,1:T(8,128)})) %all-reduce.37.cloned.1.call-update) | async-done | bytes 196624 | tf_op jit(solution)/shard_map/psum | solution.py:15
  886.1 11.7 cholesky.126
  899.2 9.8 custom-call.24
  915.3 111.7 %all-reduce.25.cloned.1.call-done = f32[1024,128]{0,1:T(8,128)} async-done(((f32[1024,128]{0,1:T(8,128)}), f32[1024,128]{0,1:T(8,128)}) %all-reduce.25.cloned.1.call-update) | async-done | bytes 524304 | tf_op jit(solution)/shard_map/psum | solution.py:15
  1028.8 73.5 %all-reduce.35.cloned.1.call-done = (f32[128,256]{0,1:T(8,128)}, f32[128,128]{0,1:T(8,128)}) async-done(((f32[128,256]{0,1:T(8,128)}, f32[128,128]{0,1:T(8,128)}), (f32[128,256]{0,1:T(8,128)}, f32[128,128]{0,1:T(8,128)})) %all-reduce.35.cloned.1.call-update) | async-done | bytes 196624 | tf_op jit(solution)/shard_map/psum | solution.py:15
  1104.1 11.7 cholesky.137
  1133.2 111.7 %all-reduce.27.cloned.1.call-done = f32[1024,128]{0,1:T(8,128)} async-done(((f32[1024,128]{0,1:T(8,128)}), f32[1024,128]{0,1:T(8,128)}) %all-reduce.27.cloned.1.call-update) | async-done | bytes 524304 | tf_op jit(solution)/shard_map/psum | solution.py:15
  1247.0 73.3 %all-reduce.33.cloned.1.call-done = (f32[128,256]{0,1:T(8,128)}, f32[128,128]{0,1:T(8,128)}) async-done(((f32[128,256]{0,1:T(8,128)}, f32[128,128]{0,1:T(8,128)}), (f32[128,256]{0,1:T(8,128)}, f32[128,128]{0,1:T(8,128)})) %all-reduce.33.cloned.1.call-update) | async-done | bytes 196624 | tf_op jit(solution)/shard_map/psum | solution.py:15
  1322.1 11.7 cholesky.148
  1351.4 111.5 %all-reduce.29.cloned.1.call-done = f32[1024,128]{0,1:T(8,128)} async-done(((f32[1024,128]{0,1:T(8,128)}), f32[1024,128]{0,1:T(8,128)}) %all-reduce.29.cloned.1.call-update) | async-done | bytes 524304 | tf_op jit(solution)/shard_map/psum | solution.py:15
  1464.5 73.8 %all-reduce.31.cloned.1.call-done = (f32[128,256]{0,1:T(8,128)}, f32[128,128]{0,1:T(8,128)}) async-done(((f32[128,256]{0,1:T(8,128)}, f32[128,128]{0,1:T(8,128)}), (f32[128,256]{0,1:T(8,128)}, f32[128,128]{0,1:T(8,128)})) %all-reduce.31.cloned.1.call-update) | async-done | bytes 196624 | tf_op jit(solution)/shard_map/psum | solution.py:15
  1540.1 11.7 cholesky.159
  (157 shorter events, 136.6 us)
Async XLA Ops:
  6.5 104.5 %all-gather.2.cloned.1.call-start = ((), (), s32[]{:S(2)}) async-start(), calls=%async_computation.1 | async-start | bytes 17039360 | tf_op jit(solution)/shard_map/all_gather | solution.py:39
  7.3 248.8 %reduce-scatter.2.cloned.1.call-start = ((), (), s32[]{:S(2)}) async-start(), calls=%async_computation.2 | async-start | bytes 5242880 | tf_op jit(solution)/shard_map/reduce_scatter | solution.py:59
  197.1 10.7 copy-start
  207.8 165.1 %all-reduce.19.cloned.1.call-start = ((), (), s32[]{:S(2)}) async-start(), calls=%async_computation.3 | async-start | bytes 1048576 | tf_op jit(solution)/shard_map/psum | solution.py:15
  258.3 190.0 %all-reduce.41.cloned.1.call-start = ((), (), s32[]{:S(2)}) async-start(), calls=%async_computation.14 | async-start | bytes 393216 | tf_op jit(solution)/shard_map/psum | solution.py:15
  374.4 216.4 %all-reduce.21.cloned.1.call-start = ((), (), s32[]{:S(2)}) async-start(), calls=%async_computation.4 | async-start | bytes 1048576 | tf_op jit(solution)/shard_map/psum | solution.py:15
  478.4 187.8 %all-reduce.39.cloned.1.call-start = ((), (), s32[]{:S(2)}) async-start(), calls=%async_computation.13 | async-start | bytes 393216 | tf_op jit(solution)/shard_map/psum | solution.py:15
  592.3 216.5 %all-reduce.23.cloned.1.call-start = ((), (), s32[]{:S(2)}) async-start(), calls=%async_computation.5 | async-start | bytes 1048576 | tf_op jit(solution)/shard_map/psum | solution.py:15
  696.4 188.0 %all-reduce.37.cloned.1.call-start = ((), (), s32[]{:S(2)}) async-start(), calls=%async_computation.12 | async-start | bytes 393216 | tf_op jit(solution)/shard_map/psum | solution.py:15
  810.3 216.6 %all-reduce.25.cloned.1.call-start = ((), (), s32[]{:S(2)}) async-start(), calls=%async_computation.6 | async-start | bytes 1048576 | tf_op jit(solution)/shard_map/psum | solution.py:15
  914.5 187.8 %all-reduce.35.cloned.1.call-start = ((), (), s32[]{:S(2)}) async-start(), calls=%async_computation.11 | async-start | bytes 393216 | tf_op jit(solution)/shard_map/psum | solution.py:15
  1028.4 216.5 %all-reduce.27.cloned.1.call-start = ((), (), s32[]{:S(2)}) async-start(), calls=%async_computation.7 | async-start | bytes 1048576 | tf_op jit(solution)/shard_map/psum | solution.py:15
  1132.5 187.8 %all-reduce.33.cloned.1.call-start = ((), (), s32[]{:S(2)}) async-start(), calls=%async_computation.10 | async-start | bytes 393216 | tf_op jit(solution)/shard_map/psum | solution.py:15
  1246.4 216.5 %all-reduce.29.cloned.1.call-start = ((), (), s32[]{:S(2)}) async-start(), calls=%async_computation.8 | async-start | bytes 1048576 | tf_op jit(solution)/shard_map/psum | solution.py:15
  1350.4 187.8 %all-reduce.31.cloned.1.call-start = ((), (), s32[]{:S(2)}) async-start(), calls=%async_computation.9 | async-start | bytes 393216 | tf_op jit(solution)/shard_map/psum | solution.py:15
Sparse Core Ops, SparseCore 0:
  10.1 100.8 all-gather.1
  207.9 48.1 reduce-scatter.1
  259.3 113.5 all-reduce.18
  375.1 73.0 all-reduce.40
  478.5 112.2 all-reduce.20
  593.1 73.0 all-reduce.38
  696.5 112.2 all-reduce.22
  811.2 73.0 all-reduce.36
  914.6 112.2 all-reduce.24
  1029.2 73.0 all-reduce.34
  1132.6 112.2 all-reduce.26
  1247.1 73.0 all-reduce.32
  1350.6 112.2 all-reduce.28
  1465.1 73.0 all-reduce.30
where the time goes:
time: 1580 us
  waiting for transfers between devices  1260 us (80%)
  other arithmetic  218 us (14%)
  local copies, waits for them, and re-layouts  55.7 us (4%)
  matrix products  23.1 us (1%)
    psum x12, waiting for transfers between devices, broadcast(): return lax.psum(kept, axis)  1110 us
    all_gather x1, waiting for transfers between devices, body(): lax.all_gather(child_tile[None], ('row', 'col'), axis=0, tiled=True)  102 us
    another operation x18, other arithmetic, body(): pivot_factor = jnp.linalg.cholesky(share_diagonal)  74.3 us
    another operation x12, other arithmetic, body(): jax.scipy.linalg.solve_triangular(pivot_factor, share_col_panel.T, lower=...  62.8 us
    scatter-add x1, other arithmetic, body(): zero_carry.at[row_target[:, :, None], :, col_target[:, None, :], :]  50.2 us
    reduce_scatter x1, waiting for transfers between devices, body(): lax.psum_scatter(spread_sum, 'sub', scatter_dimension=1, tiled=True)  47 us
  transfers between devices with their start and end apart: 14, of which 14 were waited for; matrix products, arithmetic and copies ran while one was open for 1% of the time, Pallas kernels for 0%

commit v1 on v0

v1 whole, which is shorter than its diff:
```python
import jax
import jax.numpy as jnp
from jax import lax
from jax.experimental import pallas as pl
from jax.experimental.pallas import tpu as pltpu
from jax.sharding import PartitionSpec as P

BLK = 128
NPIV = 6
PIV = NPIV * BLK

highest = lax.Precision.HIGHEST
PLANE = ("col", "sub")


def place_kernel(map_ref, row_ref, buf_ref, acc_ref):
    acc_ref[...] = jnp.zeros_like(acc_ref)
    row = row_ref[0]

    def child_row(step, carry):
        q = step // 16
        block_row = step % 16
        i = map_ref[q, block_row]

        @pl.when(i % 8 == row)
        def _():
            slot = i // 8
            for block_col in range(16):
                j = map_ref[q, block_col]
                tile = buf_ref[block_row % 8, block_col % 8, q, block_row // 8, block_col // 8]
                acc_ref[j % 8, j // 16, slot, (j // 8) % 2] += tile

        return carry

    lax.fori_loop(0, 64, child_row, 0)


def place(maps, row, buf):
    return pl.pallas_call(
        place_kernel,
        out_shape=jax.ShapeDtypeStruct((8, 4, 8, 2, 4, BLK), jnp.float32),
        in_specs=[
            pl.BlockSpec(memory_space=pltpu.SMEM),
            pl.BlockSpec(memory_space=pltpu.SMEM),
            pl.BlockSpec(memory_space=pltpu.VMEM),
        ],
        out_specs=pl.BlockSpec(memory_space=pltpu.VMEM),
        name="place",
    )(maps, row, buf)


def factor(k):
    k = [[k[i * BLK : (i + 1) * BLK, j * BLK : (j + 1) * BLK] for j in range(NPIV)] for i in range(NPIV)]
    eye = jnp.eye(BLK, dtype=jnp.float32)
    zero = jnp.zeros((BLK, BLK), jnp.float32)
    low = [[zero] * NPIV for _ in range(NPIV)]
    inv = [[zero] * NPIV for _ in range(NPIV)]
    dot = lambda a, b: jnp.dot(a, b, precision=highest)
    for b in range(NPIV):
        d = k[b][b]
        for m in range(b):
            d = d - dot(low[b][m], low[b][m].T)
        lbb = jnp.linalg.cholesky(d)
        y = jax.scipy.linalg.solve_triangular(lbb, eye, lower=True)
        low[b][b] = lbb
        inv[b][b] = y
        for i in range(b + 1, NPIV):
            x = k[i][b]
            for m in range(b):
                x = x - dot(low[i][m], low[b][m].T)
            low[i][b] = dot(x, y.T)
        for j in range(b):
            x = zero
            for m in range(j, b):
                x = x + dot(low[b][m], inv[m][j])
            inv[b][j] = -dot(y, x)
    return jnp.block(low), jnp.block(inv)


def body(front, child, child_map):
    row = lax.axis_index("row")
    col = lax.axis_index("col")
    sub = lax.axis_index("sub")
    maps = lax.all_gather(child_map[0], "sub")
    shares = child.reshape(2, 32, 4, 2, BLK).transpose(1, 0, 3, 2, 4)
    shares = lax.all_to_all(shares, PLANE, 0, 0, tiled=True)
    panel = front[:, :BLK].reshape(8, 32, 4, BLK).transpose(1, 0, 2, 3)
    panel = lax.all_to_all(panel, PLANE, 0, 0, tiled=True)
    panel = panel.reshape(8, 4, 8, 4, BLK)[:NPIV, 0]
    buf = lax.all_gather(shares, "row").reshape(8, 8, 4, 2, 2, 4, BLK)
    acc = place(maps, row[None].astype(jnp.int32), buf)
    panel = panel + acc[:NPIV, 0, :, 0]
    moved = lax.all_to_all(acc.reshape(32, 8, 2, 4, BLK), PLANE, 0, 0, tiled=True)
    matrix = front + moved.transpose(1, 0, 3, 2, 4).reshape(1024, 256)
    rows = lax.all_gather(panel, PLANE)
    rows = rows.transpose(2, 0, 3, 1, 4).reshape(1024, PIV)
    top = lax.all_gather(jnp.concatenate([rows[:BLK], matrix[:BLK]], axis=1), "row")
    top = top[:NPIV].reshape(PIV, PIV + 256)
    low, inv = factor(top[:, :PIV])
    left = jnp.dot(rows, inv.T, precision=highest)
    right = jnp.dot(inv, top[:, PIV:], precision=highest)
    piv_row = row < NPIV
    own = lax.dynamic_slice(low, (jnp.minimum(row, NPIV - 1) * BLK, 0), (BLK, PIV))
    left = left.at[:BLK].set(jnp.where(piv_row, own, left[:BLK]))
    schur = matrix - jnp.dot(left, right, precision=highest)
    schur = schur.at[:BLK].set(jnp.where(piv_row, 0.0, schur[:BLK]))
    column = lax.dynamic_slice(left, (0, jnp.minimum(col, NPIV - 1) * BLK), (1024, BLK))
    owner = (sub == 0) & (col < NPIV)
    return schur.at[:, :BLK].set(jnp.where(owner, column, schur[:, :BLK]))


def solution(mesh):
    placed = (P("row", ("col", "sub")), P("sub", "row", "col"), P("sub", None))
    return jax.shard_map(
        body, mesh=mesh, in_specs=placed, out_specs=P("row", ("col", "sub")), check_vma=False
    )
```

time: 1580 us -> 486 us (0.31)
  waiting for transfers between devices: 1260 us -> 122 us
  other arithmetic: 218 us -> 154 us
  matrix products: 23.1 us -> 85.3 us
  blocking collectives: 0 us -> 25.4 us
    psum x12 -> x0, waiting for transfers between devices: 1110 us -> none  [broadcast(): return lax.psum(kept, axis)]
    dot_general x6 -> x103, matrix products: 6.08 us -> 82.8 us  [the longest x100 63.6 us: factor(): dot = lambda a, b: jnp.dot(a, b, precision=highest)]
    scatter-add x1 -> x0, other arithmetic: 50.2 us -> none  [body(): zero_carry.at[row_target[:, :, None], :, col_target[:, None, :], :]]
    reduce_scatter x1 -> x0, waiting for transfers between devices: 47 us -> none  [body(): lax.psum_scatter(spread_sum, 'sub', scatter_dimension=1, tiled=True)]
    unnamed x4 -> x85, local copies, waits for them, and re-layouts: 5.5 us -> 29.1 us
    select_n x20 -> x1, other arithmetic: 21.8 us -> 1.91 us  [body(): left = left.at[:BLK].set(jnp.where(piv_row, own, left[:BLK]))]
    all_to_all x0 -> x2, waiting for transfers between devices: none -> 16.5 us  [the longest x1 16.5 us: body(): lax.all_to_all(acc.reshape(32, 8, 2, 4, BLK), PLANE, 0, 0, tiled=True)]
    reshape x1 -> x3, local copies, waits for them, and re-layouts: 20.8 us -> 4.37 us  [the longest x1 2.9 us: body(): acc.reshape(32, 8, 2, 4, BLK)]
  transfers between devices with their start and end apart: 14 -> 5, of which waited for: 14 -> 4; matrix products, arithmetic and copies ran while one was open for 1% -> 2% of each run, Pallas kernels for 0% -> 1%
where the time goes in v1:
time: 486 us; the launch traced here: 480 us
  other arithmetic  154 us (32%)
  waiting for transfers between devices  122 us (25%)
  matrix products  85.3 us (18%)
  local copies, waits for them, and re-layouts  59.2 us (12%)
  blocking collectives  25.4 us (5%)
  between operations  15 us (3%)
  starting transfers between devices  12.5 us (3%)
  Pallas kernels  6.25 us (1%)
    another operation x18, other arithmetic, factor(): lbb = jnp.linalg.cholesky(d)  75.5 us
    dot_general x100, matrix products, factor(): dot = lambda a, b: jnp.dot(a, b, precision=highest)  63.6 us
    another operation x6, other arithmetic, factor(): y = jax.scipy.linalg.solve_triangular(lbb, eye, lower=True)  59.5 us
    all_gather x1, waiting for transfers between devices, body(): lax.all_gather(jnp.concatenate([rows[:BLK], matrix[:BLK]], axis=1), 'row')  57.8 us
    unnamed x85, local copies, waits for them, and re-layouts  29.1 us
    all_gather x1, waiting for transfers between devices, body(): buf = lax.all_gather(shares, 'row').reshape(8, 8, 4, 2, 2, 4, BLK)  25.3 us
    all_gather x1, waiting for transfers between devices, body(): rows = lax.all_gather(panel, PLANE)  22.7 us
    all_to_all x1, waiting for transfers between devices, body(): lax.all_to_all(acc.reshape(32, 8, 2, 4, BLK), PLANE, 0, 0, tiled=True)  16.5 us
  transfers between devices with their start and end apart: 5, of which 4 were waited for; matrix products, arithmetic and copies ran while one was open for 2% of the time, Pallas kernels for 1%

profile of v1, /device:TPU:2, one launch (start us, length us, event | category | flops | bytes accessed | tf_op | source)
XLA Modules:
  0.0 479.9 jit_solution(15069634737041766309)
XLA Ops:
  7.7 15.3 %all_to_all.15 = f32[32,2,2,4,128]{4,2,3,1,0:T(2,128)S(1)} all-to-all(f32[32,2,2,4,128]{4,2,3,1,0:T(2,128)S(1)} %copy.413), channel_id=1, replica_groups=mesh['row'=8,'col'=8,'sub'=4] {'col','sub'}, dimensions={0} | all-to-all | bytes 524288 | tf_op jit(solution)/shard_map/all_to_all | solution.py:86
  24.8 5.1 %all-to-all-start.2 = ((f32[32,8,4,128]{3,2,1,0:T(4,128)}), f32[32,8,4,128]{3,2,1,0:T(4,128)S(1)}, u32[]{:S(2)}, u32[]{:S(2)}) async-start(f32[32,8,4,128]{3,2,1,0:T(4,128)} %copy.419), calls=%async_computation.2 | async-start | bytes 1048576 | tf_op jit(solution)/shard_map/all_to_all | solution.py:88
  29.9 10.1 %all-gather.2 = s32[4,1,16]{2,1,0:T(1,128)} all-gather(s32[1,1,16]{2,1,0:T(1,128)S(1)} %bitcast.304), channel_id=1, replica_groups=mesh['row'=8,'col'=8,'sub'=4] {'sub'}, dimensions={0}, use_global_device_ids=true | all-gather | bytes 320 | tf_op jit(solution)/shard_map/all_gather | solution.py:84
  40.0 25.3 %all-gather.9.cloned.1.call-done = f32[256,2,2,4,128]{4,3,2,1,0:T(4,128)} async-done(((f32[32,2,2,4,128]{4,3,2,1,0:T(4,128)}), f32[256,2,2,4,128]{4,3,2,1,0:T(4,128)}) %all-gather.9.cloned.1.call-update) | async-done | bytes 2097168 | tf_op jit(solution)/shard_map/all_gather | solution.py:90
  65.3 6.3 %place.1 = f32[8,4,8,2,4,128]{5,4,3,2,1,0:T(4,128)} custom-call(s32[4,16]{1,0:T(4,128)} %bitcast.303, s32[1]{0:T(128)} %bitcast.2.row_ref, f32[8,8,4,2,2,4,128]{6,5,4,3,2,1,0:T(4,128)} %bitcast.299), custom_call_target="tpu_custom_call" | custom-call | tf_op jit(solution)/shard_map/place/pallas_call | solution.py:39
  76.1 7.3 %all-to-all-start.1 = ((f32[32,8,2,4,128]{4,2,3,1,0:T(2,128)}), f32[32,8,2,4,128]{4,2,3,1,0:T(2,128)S(1)}, u32[]{:S(2)}, u32[]{:S(2)}) async-start(f32[32,8,2,4,128]{4,2,3,1,0:T(2,128)} %copy.415), calls=%async_computation.1 | async-start | bytes 2097152 | tf_op jit(solution)/shard_map/all_to_all | solution.py:93
  83.8 16.5 %all-to-all-done.1 = f32[32,8,2,4,128]{4,2,3,1,0:T(2,128)S(1)} async-done(((f32[32,8,2,4,128]{4,2,3,1,0:T(2,128)}), f32[32,8,2,4,128]{4,2,3,1,0:T(2,128)S(1)}, u32[]{:S(2)}, u32[]{:S(2)}) %all-to-all-start.1) | async-done | bytes 1048608 | tf_op jit(solution)/shard_map/all_to_all | solution.py:93
  103.0 22.7 %all-gather.7.cloned.1.call-done = f32[32,6,8,4,128]{4,2,3,1,0:T(8,128)} async-done(((f32[1,6,8,4,128]{4,2,3,1,0:T(8,128)}), f32[32,6,8,4,128]{4,2,3,1,0:T(8,128)}) %all-gather.7.cloned.1.call-update) | async-done | bytes 3145744 | tf_op jit(solution)/shard_map/all_gather | solution.py:95
  135.8 57.8 %all-gather.11.cloned.1.call-done = f32[1024,1024]{0,1:T(8,128)} async-done(((f32[128,1024]{0,1:T(8,128)}), f32[1024,1024]{0,1:T(8,128)}) %all-gather.11.cloned.1.call-update) | async-done | bytes 4194320 | tf_op jit(solution)/shard_map/all_gather | solution.py:97
  195.4 11.7 %cholesky.104 = f32[128,128]{1,0:T(8,128)S(1)} custom-call(f32[128,128]{1,0:T(8,128)S(1)} %fusion.46), custom_call_target="Cholesky" | custom-call | tf_op jit(solution)/shard_map/jit(cholesky)/cholesky | solution.py:63
  209.1 9.8 %custom-call.10 = f32[1,128,128]{1,2,0:T(8,128)S(1)} custom-call(f32[1,128,128]{2,1,0:T(8,128)S(1)} %get-tuple-element.55), custom_call_target="InvertDiagBlocksLowerTriangular" | custom-call | tf_op jit(solution)/shard_map/jit(_solve_triangular)/triangular_solve | solution.py:64
  226.8 11.9 %cholesky.115 = f32[128,128]{1,0:T(8,128)S(1)} custom-call(f32[128,128]{1,0:T(8,128)S(1)} %fusion.44), custom_call_target="Cholesky" | custom-call | tf_op jit(solution)/shard_map/jit(cholesky)/cholesky | solution.py:63
  241.3 9.8 %custom-call.11 = f32[1,128,128]{1,2,0:T(8,128)S(1)} custom-call(f32[1,128,128]{2,1,0:T(8,128)S(1)} %get-tuple-element.53), custom_call_target="InvertDiagBlocksLowerTriangular" | custom-call | tf_op jit(solution)/shard_map/jit(_solve_triangular)/triangular_solve | solution.py:64
  263.3 11.7 %cholesky.126 = f32[128,128]{1,0:T(8,128)S(1)} custom-call(f32[128,128]{1,0:T(8,128)S(1)} %fusion.42), custom_call_target="Cholesky" | custom-call | tf_op jit(solution)/shard_map/jit(cholesky)/cholesky | solution.py:63
  278.2 9.8 %custom-call.12 = f32[1,128,128]{1,2,0:T(8,128)S(1)} custom-call(f32[1,128,128]{2,1,0:T(8,128)S(1)} %get-tuple-element.51), custom_call_target="InvertDiagBlocksLowerTriangular" | custom-call | tf_op jit(solution)/shard_map/jit(_solve_triangular)/triangular_solve | solution.py:64
  303.2 11.7 %cholesky.137 = f32[128,128]{1,0:T(8,128)S(1)} custom-call(f32[128,128]{1,0:T(8,128)S(1)} %fusion.40), custom_call_target="Cholesky" | custom-call | tf_op jit(solution)/shard_map/jit(cholesky)/cholesky | solution.py:63
  318.7 9.8 %custom-call.13 = f32[1,128,128]{1,2,0:T(8,128)S(1)} custom-call(f32[1,128,128]{2,1,0:T(8,128)S(1)} %get-tuple-element.49), custom_call_target="InvertDiagBlocksLowerTriangular" | custom-call | tf_op jit(solution)/shard_map/jit(_solve_triangular)/triangular_solve | solution.py:64
  349.0 11.7 %cholesky.148 = f32[128,128]{1,0:T(8,128)S(1)} custom-call(f32[128,128]{1,0:T(8,128)S(1)} %fusion.38), custom_call_target="Cholesky" | custom-call | tf_op jit(solution)/shard_map/jit(cholesky)/cholesky | solution.py:63
  365.3 9.8 %custom-call.14 = f32[1,128,128]{1,2,0:T(8,128)S(1)} custom-call(f32[1,128,128]{2,1,0:T(8,128)S(1)} %get-tuple-element.47), custom_call_target="InvertDiagBlocksLowerTriangular" | custom-call | tf_op jit(solution)/shard_map/jit(_solve_triangular)/triangular_solve | solution.py:64
  399.3 12.5 %cholesky.159 = f32[128,128]{1,0:T(8,128)S(1)} custom-call(f32[128,128]{1,0:T(8,128)} %fusion.36), custom_call_target="Cholesky" | custom-call | tf_op jit(solution)/shard_map/jit(cholesky)/cholesky | solution.py:63
  421.3 10.4 %custom-call.15 = f32[1,128,128]{1,2,0:T(8,128)} custom-call(f32[1,128,128]{2,1,0:T(8,128)S(1)} %get-tuple-element.45), custom_call_target="InvertDiagBlocksLowerTriangular" | custom-call | tf_op jit(solution)/shard_map/jit(_solve_triangular)/triangular_solve | solution.py:64
  441.5 11.3 %fusion = f32[1024,768]{1,0:T(8,128)} fusion(f32[768,768]{1,0:T(8,128)S(1)} %constant_dynamic-update-slice_fusion, f32[128,8,6,128]{3,2,1,0:T(8,128)} %bitcast.290), kind=kOutput, calls=%fused_computation | convolution fusion | flops 7247757312 | bytes 8650752 | tf_op jit(solution)/shard_map/dot_general | solution.py:100
  458.3 4.0 fusion.8
  462.3 4.0 convolution_subtract_fusion
  (277 shorter events, 148.6 us)
Async XLA Ops:
  6.5 17.3 %slice-start = ((f32[1024,256]{1,0:T(8,128)}), f32[1024,128]{1,0:T(8,128)S(1)}, s32[]{:S(2)}) async-start(f32[1024,256]{1,0:T(8,128)} %param.48), calls=%async_computation.6 | async-start | bytes 1048576 | tf_op jit(solution)/shard_map/slice | solution.py:87
  6.5 58.8 %all-gather.9.cloned.1.call-start = ((), (), s32[]{:S(2)}) async-start(), calls=%async_computation.4 | async-start | bytes 2359296 | tf_op jit(solution)/shard_map/all_gather | solution.py:90
  7.7 22.2 %copy-start.15 = (s32[1,16]{1,0:T(1,128)S(1)}, s32[1,16]{1,0:T(1,128)}, u32[]{:S(2)}) copy-start(s32[1,16]{1,0:T(1,128)} %param.50) | copy-start | bytes 196
  24.8 46.8 %all-to-all-start.2 = ((f32[32,8,4,128]{3,2,1,0:T(4,128)}), f32[32,8,4,128]{3,2,1,0:T(4,128)S(1)}, u32[]{:S(2)}, u32[]{:S(2)}) async-start(f32[32,8,4,128]{3,2,1,0:T(4,128)} %copy.419), calls=%async_computation.2 | async-start | bytes 1048576 | tf_op jit(solution)/shard_map/all_to_all | solution.py:88
  29.9 95.8 %all-gather.7.cloned.1.call-start = ((), (), s32[]{:S(2)}) async-start(), calls=%async_computation.3 | async-start | bytes 3244032 | tf_op jit(solution)/shard_map/all_gather | solution.py:95
  71.5 11.9 %copy-start.4 = (f32[1024,256]{1,0:T(8,128)S(1)}, f32[1024,256]{1,0:T(8,128)}, u32[]{:S(2)}) copy-start(f32[1024,256]{1,0:T(8,128)} %param.48) | copy-start | bytes 3145732
  76.1 24.2 %all-to-all-start.1 = ((f32[32,8,2,4,128]{4,2,3,1,0:T(2,128)}), f32[32,8,2,4,128]{4,2,3,1,0:T(2,128)S(1)}, u32[]{:S(2)}, u32[]{:S(2)}) async-start(f32[32,8,2,4,128]{4,2,3,1,0:T(2,128)} %copy.415), calls=%async_computation.1 | async-start | bytes 2097152 | tf_op jit(solution)/shard_map/all_to_all | solution.py:93
  83.4 110.2 %all-gather.11.cloned.1.call-start = ((), (), s32[]{:S(2)}) async-start(), calls=%async_computation.5 | async-start | bytes 4718592 | tf_op jit(solution)/shard_map/all_gather | solution.py:97
  101.4 1.0 copy-start.1
  125.7 6.3 %copy-start.3 = (f32[32,6,8,4,128]{4,2,3,1,0:T(8,128)S(1)}, f32[32,6,8,4,128]{4,2,3,1,0:T(8,128)}, u32[]{:S(2)}) copy-start(f32[32,6,8,4,128]{4,2,3,1,0:T(8,128)} %all-gather.7.cloned.1.call-done) | copy-start | bytes 9437188
  379.1 11.4 %copy-start.10 = (f32[128,128]{1,0:T(8,128)S(1)}, f32[128,128]{1,0:T(8,128)}, u32[]{:S(2)}) copy-start(f32[128,128]{1,0:T(8,128)} %fusion.67) | copy-start | bytes 196612
  381.3 12.0 %copy-start.9 = (f32[128,128]{1,0:T(8,128)S(1)}, f32[128,128]{1,0:T(8,128)}, u32[]{:S(2)}) copy-start(f32[128,128]{1,0:T(8,128)} %fusion.68) | copy-start | bytes 196612
  381.9 12.8 %copy-start.11 = (f32[128,128]{1,0:T(8,128)S(1)}, f32[128,128]{1,0:T(8,128)}, u32[]{:S(2)}) copy-start(f32[128,128]{1,0:T(8,128)} %fusion.69) | copy-start | bytes 196612
  383.9 11.6 %copy-start.12 = (f32[128,128]{1,0:T(8,128)S(1)}, f32[128,128]{1,0:T(8,128)}, u32[]{:S(2)}) copy-start(f32[128,128]{1,0:T(8,128)} %copy.465) | copy-start | bytes 196612
  392.3 42.3 %copy-start.7 = (f32[128,128]{1,0:T(8,128)S(1)}, f32[128,128]{1,0:T(8,128)}, u32[]{:S(2)}) copy-start(f32[128,128]{1,0:T(8,128)} %fusion.75) | copy-start | bytes 196612
  393.7 41.4 %copy-start.8 = (f32[128,128]{1,0:T(8,128)S(1)}, f32[128,128]{1,0:T(8,128)}, u32[]{:S(2)}) copy-start(f32[128,128]{1,0:T(8,128)} %fusion.76) | copy-start | bytes 196612
  395.6 40.0 %copy-start.14 = (f32[128,128]{1,0:T(8,128)S(1)}, f32[128,128]{1,0:T(8,128)}, u32[]{:S(2)}) copy-start(f32[128,128]{1,0:T(8,128)} %get-tuple-element.69) | copy-start | bytes 196612
  398.3 40.7 %copy-start.6 = (f32[128,128]{1,0:T(8,128)S(1)}, f32[128,128]{1,0:T(8,128)}, u32[]{:S(2)}) copy-start(f32[128,128]{1,0:T(8,128)} %fusion.77) | copy-start | bytes 196612
  398.3 40.7 %copy-start.13 = (f32[128,128]{1,0:T(8,128)S(1)}, f32[128,128]{1,0:T(8,128)}, u32[]{:S(2)}) copy-start(f32[128,128]{1,0:T(8,128)} %get-tuple-element.75) | copy-start | bytes 196612
  398.7 40.9 %copy-start.5 = (f32[128,128]{1,0:T(8,128)S(1)}, f32[128,128]{1,0:T(8,128)}, u32[]{:S(2)}) copy-start(f32[128,128]{1,0:T(8,128)} %fusion.78) | copy-start | bytes 196612
  439.9 1.5 copy-start
  458.2 4.0 copy-start.2
Sparse Core Ops, SparseCore 0:
  23.9 41.3 all-gather.8
  73.4 52.2 all-gather.6
  131.2 62.3 all-gather.10

commit v2 on v1

v2 whole, which is shorter than its diff:
```python
import jax
import jax.numpy as jnp
from jax import lax
from jax.experimental import pallas as pl
from jax.experimental.pallas import tpu as pltpu
from jax.sharding import PartitionSpec as P

BLK = 128
NPIV = 6
PIV = NPIV * BLK
PLANE = ("col", "sub")
HI = lax.Precision.HIGHEST
VM = pl.BlockSpec(memory_space=pltpu.VMEM)
SM = pl.BlockSpec(memory_space=pltpu.SMEM)


def nt(a, b, precision=HI):
    return lax.dot_general(a, b, (((1,), (1,)), ((), ())), precision=precision, preferred_element_type=jnp.float32)
def tn(a, b, precision=HI):
    return lax.dot_general(a, b, (((0,), (0,)), ((), ())), precision=precision, preferred_element_type=jnp.float32)

def rsqrt(x):
    return lax.rsqrt(x)

def eliminate(a_ref):
    sub = lax.broadcasted_iota(jnp.int32, (8, 256), 0)
    for g in range(16):
        rows = a_ref[8 * g : 8 * g + 8, :]
        left = rows[:, :BLK]
        e = {}
        for j in range(8):
            c = jnp.broadcast_to(left[:, 8 * g + j : 8 * g + j + 1], (8, BLK))
            for i in range(j, 8):
                e[j, i] = jnp.broadcast_to(c[i : i + 1, :], (8, BLK))
        r = [jnp.broadcast_to(rows[i : i + 1, :], (8, 256)) for i in range(8)]
        out = None
        for j in range(8):
            s = rsqrt(e[j, j])
            u = {i: e[j, i] * s for i in range(j + 1, 8)}
            for i in range(j + 1, 8):
                for m in range(i, 8):
                    e[i, m] = e[i, m] - u[i] * u[m]
            rj = r[j] * jnp.concatenate([s, s], axis=1)
            for i in range(j + 1, 8):
                r[i] = r[i] - jnp.concatenate([u[i], u[i]], axis=1) * rj
            out = rj if out is None else jnp.where(sub == j, rj, out)
        a_ref[8 * g : 8 * g + 8, :] = out
        if g < 15:
            t = tn(out[:, :BLK], out)
            a_ref[8 * g + 8 :, :] = a_ref[8 * g + 8 :, :] - t[8 * g + 8 :, :]

def factor_kernel(k_ref, l_ref, y_ref, a_ref, m_ref):
    eye = (lax.broadcasted_iota(jnp.int32, (BLK, BLK), 0) == lax.broadcasted_iota(jnp.int32, (BLK, BLK), 1)).astype(jnp.float32)
    low = lax.broadcasted_iota(jnp.int32, (BLK, BLK), 0) >= lax.broadcasted_iota(jnp.int32, (BLK, BLK), 1)
    m_ref[...] = k_ref[...]
    l_ref[...] = jnp.zeros_like(l_ref)
    def step(b, carry):
        at = pl.ds(pl.multiple_of(b * BLK, BLK), BLK)
        a_ref[:, :BLK] = m_ref[at, at]
        a_ref[:, BLK:] = eye
        eliminate(a_ref)
        y = a_ref[:, BLK:]
        y_ref[b] = y
        l_ref[at, at] = jnp.where(low, a_ref[:, :BLK].T, 0.0)
        def solve(i, c):
            rows = pl.ds(pl.multiple_of(i * BLK, BLK), BLK)
            l_ref[rows, at] = nt(m_ref[rows, at], y)
            return c
        lax.fori_loop(b + 1, NPIV, solve, 0)
        def update(i, c):
            rows = pl.ds(pl.multiple_of(i * BLK, BLK), BLK)
            m_ref[rows, :] = m_ref[rows, :] - nt(l_ref[rows, at], l_ref[:, at])
            return c
        lax.fori_loop(b + 1, NPIV, update, 0)
        return carry
    lax.fori_loop(0, NPIV, step, 0)

def factor(k):
    return pl.pallas_call(
        factor_kernel,
        out_shape=(jax.ShapeDtypeStruct((PIV, PIV), jnp.float32), jax.ShapeDtypeStruct((NPIV, BLK, BLK), jnp.float32)),
        in_specs=[pl.BlockSpec(memory_space=pltpu.VMEM)],
        out_specs=(pl.BlockSpec(memory_space=pltpu.VMEM),)*2,
        scratch_shapes=[pltpu.VMEM((BLK, 256), jnp.float32), pltpu.VMEM((PIV, PIV), jnp.float32)],
        cost_estimate=pl.CostEstimate(flops=60_000_000_000, bytes_accessed=200_000_000, transcendentals=0),
        name="factor",
    )(k)


def split(x):
    high = x.astype(jnp.bfloat16)
    return high, (x - high.astype(jnp.float32)).astype(jnp.bfloat16)


def dot3(a, b, dims):
    def one(x, y):
        return lax.dot_general(x, y, (dims, ((), ())), preferred_element_type=jnp.float32)

    return one(a[0], b[0]) + (one(a[0], b[1]) + one(a[1], b[0]))


NT = ((1,), (1,))
NN = ((1,), (0,))


def schur_kernel(
    where_ref, rows_ref, top_ref, matrix_ref, low_ref, inv_ref, out_ref,
    lh, ll, yh, yl, uh, ul, x_ref,
):
    tile = pl.program_id(0)
    row, col, sub = where_ref[0], where_ref[1], where_ref[2]

    @pl.when(tile == 0)
    def _():
        high, rest = split(low_ref[...])
        lh[...] = high
        ll[...] = rest
        zero = jnp.zeros((BLK, BLK), jnp.float32)
        for p in range(3):
            first, second = inv_ref[2 * p], inv_ref[2 * p + 1]
            at = 256 * p
            cross = jnp.dot(low_ref[at + BLK : at + 256, at : at + BLK], first, precision=HI)
            cross = -jnp.dot(second, cross, precision=HI)
            pair = jnp.concatenate(
                [jnp.concatenate([first, zero], axis=1), jnp.concatenate([cross, second], axis=1)], axis=0
            )
            high, rest = split(pair)
            yh[p] = high
            yl[p] = rest
        for p in range(3):
            at = 256 * p
            x = top_ref[at : at + 256, :]
            if p:
                x = x - dot3((lh[at : at + 256, :at], ll[at : at + 256, :at]), (uh[:at, :], ul[:at, :]), NN)
            high, rest = split(dot3((yh[p], yl[p]), split(x), NN))
            uh[at : at + 256, :] = high
            ul[at : at + 256, :] = rest

    acc = matrix_ref[...]
    xs = []
    for p in range(3):
        at = 256 * p
        x = rows_ref[:, at : at + 256]
        for m in range(p):
            cut = slice(256 * m, 256 * m + 256)
            x = x - dot3(xs[m], (lh[at : at + 256, cut], ll[at : at + 256, cut]), NT)
        x = dot3(split(x), (yh[p], yl[p]), NT)
        x_ref[:, at : at + 256] = x
        xs.append(split(x))
        acc = acc - dot3(xs[p], (uh[at : at + 256, :], ul[at : at + 256, :]), NN)
    out_ref[...] = acc

    @pl.when((tile == 0) & (row < NPIV))
    def _():
        out_ref[:BLK, :] = jnp.zeros((BLK, 256), jnp.float32)
        x_ref[:BLK, :] = low_ref[pl.ds(pl.multiple_of(row * BLK, BLK), BLK), :]

    @pl.when((sub == 0) & (col < NPIV))
    def _():
        out_ref[:, :BLK] = x_ref[:, pl.ds(pl.multiple_of(col * BLK, BLK), BLK)]


def schur(where, rows, top, matrix, low, inv):
    whole = lambda shape: pl.BlockSpec(shape, lambda t: (0,) * len(shape), pipeline_mode=pl.Buffered(1))
    return pl.pallas_call(
        schur_kernel,
        out_shape=jax.ShapeDtypeStruct((1024, 256), jnp.float32),
        grid=(4,),
        in_specs=[
            SM,
            pl.BlockSpec((256, PIV), lambda t: (t, 0)),
            whole((PIV, 256)),
            pl.BlockSpec((256, 256), lambda t: (t, 0)),
            whole((PIV, PIV)),
            whole((NPIV, BLK, BLK)),
        ],
        out_specs=pl.BlockSpec((256, 256), lambda t: (t, 0)),
        scratch_shapes=[
            pltpu.VMEM((PIV, PIV), jnp.bfloat16),
            pltpu.VMEM((PIV, PIV), jnp.bfloat16),
            pltpu.VMEM((3, 256, 256), jnp.bfloat16),
            pltpu.VMEM((3, 256, 256), jnp.bfloat16),
            pltpu.VMEM((PIV, 256), jnp.bfloat16),
            pltpu.VMEM((PIV, 256), jnp.bfloat16),
            pltpu.VMEM((256, PIV), jnp.float32),
        ],
        name="schur",
    )(where, rows, top, matrix, low, inv)


def place_kernel(map_ref, where_ref, buf_ref, acc_ref):
    acc_ref[...] = jnp.zeros_like(acc_ref)
    row = where_ref[0]

    def child_row(step, carry):
        q = step // 16
        block_row = step % 16
        i = map_ref[q, block_row]

        @pl.when(i % 8 == row)
        def _():
            slot = i // 8
            for block_col in range(16):
                j = map_ref[q, block_col]
                tile = buf_ref[block_row % 8, block_col % 8, q, block_row // 8, block_col // 8]
                acc_ref[j % 8, j // 16, slot, (j // 8) % 2] += tile

        return carry

    lax.fori_loop(0, 64, child_row, 0)


def place(maps, where, buf):
    return pl.pallas_call(
        place_kernel,
        out_shape=jax.ShapeDtypeStruct((8, 4, 8, 2, 4, BLK), jnp.float32),
        in_specs=[SM, SM, VM],
        out_specs=VM,
        name="place",
    )(maps, where, buf)


def place_pivot_kernel(map_ref, buf_ref, acc_ref):
    for i in range(NPIV):
        for j in range(NPIV):
            acc_ref[i, j] = buf_ref[i, 32 + j]

    def child_row(step, carry):
        q = step // NPIV
        block_row = step % NPIV
        i = map_ref[q, block_row]

        @pl.when(i < NPIV)
        def _():
            for block_col in range(NPIV):
                j = map_ref[q, block_col]

                @pl.when(j < NPIV)
                def _():
                    acc_ref[i, j] += buf_ref[block_row, block_col * 4 + q]

        return carry

    lax.fori_loop(0, 4 * NPIV, child_row, 0)


def place_pivot(maps, buf):
    return pl.pallas_call(
        place_pivot_kernel,
        out_shape=jax.ShapeDtypeStruct((NPIV, NPIV, 4, BLK), jnp.float32),
        in_specs=[SM, VM],
        out_specs=VM,
        name="place_pivot",
    )(maps, buf)


def body(front, child, child_map):
    where = jnp.stack([lax.axis_index(a) for a in ("row", "col", "sub")]).astype(jnp.int32)
    maps = lax.all_gather(child_map[0], "sub")
    shares = child.reshape(2, 32, 4, 2, BLK).transpose(1, 0, 3, 2, 4)
    shares = lax.all_to_all(shares, PLANE, 0, 0, tiled=True)
    panel = front[:, :BLK].reshape(8, 32, 4, BLK).transpose(1, 0, 2, 3)
    panel = lax.all_to_all(panel, PLANE, 0, 0, tiled=True)
    panel = panel.reshape(8, 4, 8, 4, BLK)[:NPIV, 0]
    pivot = jnp.concatenate([shares[:, 0, 0], panel[:, 0]], axis=0)
    pivot = place_pivot(maps, lax.all_gather(pivot, "row"))
    k = lax.all_gather(pivot, PLANE).transpose(1, 0, 3, 2, 4).reshape(PIV, PIV)
    shares, _ = lax.optimization_barrier((shares, pivot))
    low, inv = factor(k)
    buf = lax.all_gather(shares, "row").reshape(8, 8, 4, 2, 2, 4, BLK)
    acc = place(maps, where, buf)
    panel = panel + acc[:NPIV, 0, :, 0]
    rows = lax.all_gather(panel, PLANE)
    rows = rows.transpose(2, 0, 3, 1, 4).reshape(1024, PIV)
    moved = lax.all_to_all(acc.reshape(32, 8, 2, 4, BLK), PLANE, 0, 0, tiled=True)
    matrix = front + moved.transpose(1, 0, 3, 2, 4).reshape(1024, 256)
    top = lax.all_gather(matrix[:BLK], "row")[:NPIV].reshape(PIV, 256)
    return schur(where, rows, top, matrix, low, inv)


def solution(mesh):
    placed = (P("row", ("col", "sub")), P("sub", "row", "col"), P("sub", None))
    return jax.shard_map(
        body, mesh=mesh, in_specs=placed, out_specs=P("row", ("col", "sub")), check_vma=False
    )
```

time: 486 us -> 289 us (0.59)
  other arithmetic: 154 us -> 1.67 us
  matrix products: 85.3 us -> 0 us
  Pallas kernels: 6.25 us -> 91.3 us
  waiting for transfers between devices: 122 us -> 82.1 us
  blocking collectives: 25.4 us -> 65 us
  local copies, waits for them, and re-layouts: 59.2 us -> 20.7 us
    another operation x25 -> x1, other arithmetic: 136 us -> 0.59 us  [body(): jnp.stack([lax.axis_index(a) for a in ('row', 'col', 'sub')])]
    pallas_call x0 -> x3, Pallas kernels: none -> 84.6 us  [the longest x1 68.2 us: factor(): pl.pallas_call(factor_kernel, out_shape=(jax.ShapeDtypeStruct((PIV, PIV),...]
    dot_general x103 -> x0, matrix products: 82.8 us -> none  [the longest x100 63.6 us: factor(): dot = lambda a, b: jnp.dot(a, b, precision=highest)]
    all_gather x1 -> x2, waiting for transfers between devices: 57.8 us -> 19.7 us  [the longest x1 19.7 us: body(): k = lax.all_gather(pivot, PLANE).transpose(1, 0, 3, 2, 4).reshape(PIV, PIV)]
    all_gather x0 -> x1, blocking collectives: none -> 31.3 us  [body(): pivot = place_pivot(maps, lax.all_gather(pivot, 'row'))]
    unnamed x85 -> x8, local copies, waits for them, and re-layouts: 29.1 us -> 4.35 us
    all_gather x1, waiting for transfers between devices: 25.3 us -> 38.6 us  [body(): buf = lax.all_gather(shares, 'row').reshape(8, 8, 4, 2, 2, 4, BLK)]
    all_to_all x1, waiting for transfers between devices: 16.5 us -> 5.85 us  [body(): shares = lax.all_to_all(shares, PLANE, 0, 0, tiled=True)]
  transfers between devices with their start and end apart: 5 -> 6, of which waited for: 4 -> 5; matrix products, arithmetic and copies ran while one was open for 2% -> 5% of each run, Pallas kernels for 1% -> 26%
where the time goes in v2:
time: 289 us; the launch traced here: 287 us
  Pallas kernels  91.3 us (32%)
  waiting for transfers between devices  82.1 us (28%)
  blocking collectives  65 us (22%)
  local copies, waits for them, and re-layouts  20.7 us (7%)
  between operations  13.3 us (5%)
  starting transfers between devices  12.9 us (4%)
    pallas_call x1, Pallas kernels, factor(): pl.pallas_call(factor_kernel, out_shape=(jax.ShapeDtypeStruct((PIV, PIV),...  68.2 us
    all_gather x1, waiting for transfers between devices, body(): buf = lax.all_gather(shares, 'row').reshape(8, 8, 4, 2, 2, 4, BLK)  38.6 us
    all_gather x1, blocking collectives, body(): pivot = place_pivot(maps, lax.all_gather(pivot, 'row'))  31.3 us
    all_to_all x1, blocking collectives, body(): lax.all_to_all(acc.reshape(32, 8, 2, 4, BLK), PLANE, 0, 0, tiled=True)  23.8 us
    all_gather x1, waiting for transfers between devices, body(): k = lax.all_gather(pivot, PLANE).transpose(1, 0, 3, 2, 4).reshape(PIV, PIV)  19.7 us
    all_gather x1, waiting for transfers between devices, body(): rows = lax.all_gather(panel, PLANE)  16.8 us
    pallas_call x1, Pallas kernels, schur(): pl.pallas_call(schur_kernel, out_shape=jax.ShapeDtypeStruct((1024, 256),...  13.6 us
    all_gather x1, blocking collectives, body(): maps = lax.all_gather(child_map[0], 'sub')  9.93 us
  transfers between devices with their start and end apart: 6, of which 5 were waited for; matrix products, arithmetic and copies ran while one was open for 5% of the time, Pallas kernels for 26%

profile of v2, /device:TPU:2, one launch (start us, length us, event | category | flops | bytes accessed | tf_op | source)
XLA Modules:
  0.0 286.9 jit_solution(2888546432305117018)
XLA Ops:
  6.5 1.1 reshape.46
  8.3 7.6 %all-to-all-start.1 = ((f32[32,2,2,4,128]{4,2,3,1,0:T(2,128)}), f32[32,2,2,4,128]{4,2,3,1,0:T(2,128)S(1)}, u32[]{:S(2)}, u32[]{:S(2)}) async-start(f32[32,2,2,4,128]{4,2,3,1,0:T(2,128)} %copy.40), calls=%async_computation.1 | async-start | bytes 524288 | tf_op jit(solution)/shard_map/all_to_all | solution.py:261
  16.0 1.1 slice.21
  17.1 0.9 copy.37
  18.0 5.8 %all-to-all-done.1 = f32[32,2,2,4,128]{4,2,3,1,0:T(2,128)S(1)} async-done(((f32[32,2,2,4,128]{4,2,3,1,0:T(2,128)}), f32[32,2,2,4,128]{4,2,3,1,0:T(2,128)S(1)}, u32[]{:S(2)}, u32[]{:S(2)}) %all-to-all-start.1) | async-done | bytes 262176 | tf_op jit(solution)/shard_map/all_to_all | solution.py:261
  23.8 5.1 %all-to-all-start = ((f32[32,8,4,128]{3,2,1,0:T(4,128)}), f32[32,8,4,128]{3,2,1,0:T(4,128)S(1)}, u32[]{:S(2)}, u32[]{:S(2)}) async-start(f32[32,8,4,128]{3,2,1,0:T(4,128)} %copy.37), calls=%async_computation | async-start | bytes 1048576 | tf_op jit(solution)/shard_map/all_to_all | solution.py:263
  29.0 9.9 %all-gather.4 = s32[4,1,16]{2,1,0:T(1,128)} all-gather(s32[1,1,16]{2,1,0:T(1,128)S(1)} %bitcast.63), channel_id=1, replica_groups=mesh['row'=8,'col'=8,'sub'=4] {'sub'}, dimensions={0}, use_global_device_ids=true | all-gather | bytes 320 | tf_op jit(solution)/shard_map/all_gather | solution.py:259
  39.5 31.3 %all-gather = f32[304,4,128]{2,1,0:T(4,128)} all-gather(f32[38,4,128]{2,1,0:T(4,128)S(1)} %pad_maximum_fusion), channel_id=2, replica_groups=mesh['row'=8,'col'=8,'sub'=4] {'row'}, dimensions={0}, use_global_device_ids=true | all-gather | bytes 700416 | tf_op jit(solution)/shard_map/all_gather | solution.py:266
  70.8 2.9 %place_pivot.1 = f32[6,6,4,128]{3,2,1,0:T(4,128)} custom-call(s32[4,16]{1,0:T(4,128)} %bitcast.61, f32[8,38,4,128]{3,2,1,0:T(4,128)} %bitcast.52), custom_call_target="tpu_custom_call" | custom-call | tf_op jit(solution)/shard_map/place_pivot/pallas_call | solution.py:248
  73.7 0.8 copy.41
  75.9 38.6 %all-gather.12.cloned.1.call-done = f32[256,2,2,4,128]{4,3,2,1,0:T(4,128)} async-done(((f32[32,2,2,4,128]{4,3,2,1,0:T(4,128)}), f32[256,2,2,4,128]{4,3,2,1,0:T(4,128)}) %all-gather.12.cloned.1.call-update) | async-done | bytes 2097168 | tf_op jit(solution)/shard_map/all_gather | solution.py:270
  114.5 6.7 %place.1 = f32[8,4,8,2,4,128]{5,4,3,2,1,0:T(4,128)} custom-call(s32[4,16]{1,0:T(4,128)} %bitcast.62, s32[3]{0:T(128)} %pad_add_fusion.where_ref, f32[8,8,4,2,2,4,128]{6,5,4,3,2,1,0:T(4,128)} %bitcast.55), custom_call_target="tpu_custom_call" | custom-call | tf_op jit(solution)/shard_map/place/pallas_call | solution.py:214
  121.1 1.9 copy.44
  123.0 23.8 %all_to_all.15 = f32[32,8,2,4,128]{4,2,3,1,0:T(2,128)S(1)} all-to-all(f32[32,8,2,4,128]{4,2,3,1,0:T(2,128)S(1)} %copy.44), channel_id=1, replica_groups=mesh['row'=8,'col'=8,'sub'=4] {'col','sub'}, dimensions={0} | all-to-all | bytes 2097152 | tf_op jit(solution)/shard_map/all_to_all | solution.py:275
  148.2 0.9 fusion
  149.8 19.7 %all-gather.16.cloned.1.call-done = f32[192,6,4,128]{3,2,1,0:T(4,128)} async-done(((f32[6,6,4,128]{3,2,1,0:T(4,128)}), f32[192,6,4,128]{3,2,1,0:T(4,128)}) %all-gather.16.cloned.1.call-update) | async-done | bytes 2359312 | tf_op jit(solution)/shard_map/all_gather | solution.py:267
  169.5 2.2 copy.46
  171.7 1.9 copy.57
  173.6 68.2 %factor.1 = (f32[768,768]{1,0:T(8,128)}, f32[6,128,128]{2,1,0:T(8,128)}) custom-call(f32[768,768]{1,0:T(8,128)} %bitcast.54), custom_call_target="tpu_custom_call" | custom-call | flops 60000002048 | bytes 200000000 | tf_op jit(solution)/shard_map/factor/pallas_call | solution.py:79
  241.8 2.1 slice.34.top_ref
  243.9 16.8 %all-gather.10.cloned.1.call-done = f32[32,6,8,4,128]{4,2,3,1,0:T(8,128)} async-done(((f32[1,6,8,4,128]{4,2,3,1,0:T(8,128)}), f32[32,6,8,4,128]{4,2,3,1,0:T(8,128)}) %all-gather.10.cloned.1.call-update) | async-done | bytes 3145744 | tf_op jit(solution)/shard_map/all_gather | solution.py:273
  260.7 3.8 %copy.43 = f32[8,32,4,6,128]{4,3,2,1,0:T(8,128)S(1)} copy(f32[8,32,4,6,128]{4,0,2,3,1:T(8,128)} %bitcast.51) | data formatting | bytes 6291456 | tf_op jit(solution)/shard_map/transpose | solution.py:274
  264.5 2.4 copy.56
  266.9 13.6 %schur.1 = f32[1024,256]{1,0:T(8,128)} custom-call(s32[3]{0:T(128)} %pad_add_fusion.where_ref, f32[1024,768]{1,0:T(8,128)} %bitcast.46, f32[768,256]{1,0:T(8,128)} %slice.34.top_ref, f32[1024,256]{1,0:T(8,128)} %copy-done, f32[768,768]{1,0:T(8,128)} %get-tuple-element.9.low_ref, f32[6,128,128]{2,1,0:T(8,128)} %get-tuple-element.10.inv_ref), custom_call_target="tpu_custom_call" | custom-call | tf_op jit(solution)/shard_map/schur/pallas_call | solution.py:165
  (26 shorter events, 4.7 us)
Async XLA Ops:
  6.5 22.5 %copy-start.2 = (s32[1,16]{1,0:T(1,128)S(1)}, s32[1,16]{1,0:T(1,128)}, u32[]{:S(2)}) copy-start(s32[1,16]{1,0:T(1,128)} %param.5) | copy-start | bytes 196
  8.3 15.5 %all-to-all-start.1 = ((f32[32,2,2,4,128]{4,2,3,1,0:T(2,128)}), f32[32,2,2,4,128]{4,2,3,1,0:T(2,128)S(1)}, u32[]{:S(2)}, u32[]{:S(2)}) async-start(f32[32,2,2,4,128]{4,2,3,1,0:T(2,128)} %copy.40), calls=%async_computation.1 | async-start | bytes 524288 | tf_op jit(solution)/shard_map/all_to_all | solution.py:261
  23.8 15.6 %all-to-all-start = ((f32[32,8,4,128]{3,2,1,0:T(4,128)}), f32[32,8,4,128]{3,2,1,0:T(4,128)S(1)}, u32[]{:S(2)}, u32[]{:S(2)}) async-start(f32[32,8,4,128]{3,2,1,0:T(4,128)} %copy.37), calls=%async_computation | async-start | bytes 1048576 | tf_op jit(solution)/shard_map/all_to_all | solution.py:263
  28.9 85.5 %all-gather.12.cloned.1.call-start = ((), (), s32[]{:S(2)}) async-start(), calls=%async_computation.4 | async-start | bytes 2359296 | tf_op jit(solution)/shard_map/all_gather | solution.py:270
  74.5 95.0 %all-gather.16.cloned.1.call-start = ((), (), s32[]{:S(2)}) async-start(), calls=%async_computation.6 | async-start | bytes 2433024 | tf_op jit(solution)/shard_map/all_gather | solution.py:267
  75.2 166.5 %all-gather.14.cloned.1.call-start = ((), (), s32[]{:S(2)}) async-start(), calls=%async_computation.5 | async-start | bytes 1179648 | tf_op jit(solution)/shard_map/all_gather | solution.py:277
  121.1 26.1 %copy-start.1 = (f32[1024,256]{1,0:T(8,128)S(1)}, f32[1024,256]{1,0:T(8,128)}, u32[]{:S(2)}) copy-start(f32[1024,256]{1,0:T(8,128)} %param.3) | copy-start | bytes 3145732
  147.4 24.3 %copy-start = (f32[1024,256]{1,0:T(8,128)}, f32[1024,256]{1,0:T(8,128)S(1)}, u32[]{:S(2)}) copy-start(f32[1024,256]{1,0:T(8,128)S(1)} %bitcast_add_fusion.matrix_ref) | copy-start | bytes 3145732
  148.1 112.5 %all-gather.10.cloned.1.call-start = ((), (), s32[]{:S(2)}) async-start(), calls=%async_computation.3 | async-start | bytes 3244032 | tf_op jit(solution)/shard_map/all_gather | solution.py:273
Sparse Core Ops, SparseCore 0:
  74.6 39.8 all-gather.11
  117.1 52.3 all-gather.15
  171.3 38.3 all-gather.13
  212.1 48.4 all-gather.9

commit v3 on v2

--- a/solution.py
+++ b/solution.py
@@ -52,7 +52,9 @@
 def factor_kernel(k_ref, l_ref, y_ref, a_ref, m_ref):
     eye = (lax.broadcasted_iota(jnp.int32, (BLK, BLK), 0) == lax.broadcasted_iota(jnp.int32, (BLK, BLK), 1)).astype(jnp.float32)
     low = lax.broadcasted_iota(jnp.int32, (BLK, BLK), 0) >= lax.broadcasted_iota(jnp.int32, (BLK, BLK), 1)
-    m_ref[...] = k_ref[...]
+    for i in range(NPIV):
+        for j in range(i + 1):
+            m_ref[i * BLK : (i + 1) * BLK, j * BLK : (j + 1) * BLK] = k_ref[i * (i + 1) // 2 + j]
     l_ref[...] = jnp.zeros_like(l_ref)
     def step(b, carry):
         at = pl.ds(pl.multiple_of(b * BLK, BLK), BLK)
@@ -85,6 +87,199 @@
         cost_estimate=pl.CostEstimate(flops=60_000_000_000, bytes_accessed=200_000_000, transcendentals=0),
         name="factor",
     )(k)
+
+
+MESH = pl.DeviceIdType.MESH
+TILES = [(i, j) for i in range(NPIV) for j in range(i + 1)]
+NT_ = len(TILES)
+
+
+def pivot_kernel(child_ref, front_ref, map_ref, k_ref, maps_ref, z_ref, acc_ref, send, got, z_got, k_got, p_got):
+    r, c, s = lax.axis_index("row"), lax.axis_index("col"), lax.axis_index("sub")
+    e = c * 4 + s
+    x, core = c // 2, c % 2
+    chip = x * 4 + s
+    partner = (r, x * 2 + 1 - core, s)
+
+    def plane_peer(d):
+        p = (e + d) % 32
+        return p, (r, p // 4, p % 4)
+
+    def chip_peer(d):
+        p = (chip + d) % 16
+        c2 = (p // 4) * 2 + core
+        return c2 * 4 + p % 4, (r, c2, p % 4)
+
+    barrier = pltpu.get_barrier_semaphore()
+
+    def greet_plane(d, carry):
+        pl.semaphore_signal(barrier, inc=1, device_id=plane_peer(d)[1], device_id_type=MESH)
+        return carry
+
+    def greet_row(d, carry):
+        pl.semaphore_signal(barrier, inc=1, device_id=((r + d) % 8, c, s), device_id_type=MESH)
+        return carry
+
+    lax.fori_loop(1, 32, greet_plane, 0)
+    lax.fori_loop(1, 8, greet_row, 0)
+    pl.semaphore_wait(barrier, 38)
+
+    def push(src, dst, ssem, rsem, device):
+        return pltpu.make_async_remote_copy(
+            src_ref=src, dst_ref=dst, send_sem=ssem, recv_sem=rsem, device_id=device, device_id_type=MESH
+        )
+
+    has_child = (r < NPIV) & (c < NPIV)
+    has_front = has_child & (s == 0)
+    spot = jnp.minimum(r, NPIV - 1)
+    seat = jnp.minimum(c, NPIV - 1)
+
+    def child_copy(d):
+        p, device = plane_peer(d)
+        return push(child_ref.at[p], z_ref.at[spot, s * 6 + seat], send.at[0], got.at[0], device)
+
+    def front_copy(d):
+        p, device = plane_peer(d)
+        return push(front_ref.at[p], z_ref.at[spot, 24 + seat], send.at[1], got.at[1], device)
+
+    def map_copy(d):
+        return push(map_ref, maps_ref.at[s], send.at[2], got.at[2], (r, c, (s + d) % 4))
+
+    own_child = pltpu.make_async_copy(child_ref.at[e], z_ref.at[spot, s * 6 + seat], got.at[0])
+    own_front = pltpu.make_async_copy(front_ref.at[e], z_ref.at[spot, 24 + seat], got.at[1])
+    own_map = pltpu.make_async_copy(map_ref, maps_ref.at[s], got.at[2])
+
+    @pl.when(has_child)
+    def _():
+        own_child.start()
+
+        def one(d, carry):
+            child_copy(d).start()
+            return carry
+
+        lax.fori_loop(1, 32, one, 0)
+
+    @pl.when(has_front)
+    def _():
+        own_front.start()
+
+        def one(d, carry):
+            front_copy(d).start()
+            return carry
+
+        lax.fori_loop(1, 32, one, 0)
+
+    own_map.start()
+    for d in range(1, 4):
+        map_copy(d).start()
+
+    def z_copy(d):
+        return push(z_ref.at[spot], z_ref.at[spot], send.at[3], z_got.at[spot], ((r + d) % 8, c, s))
+
+    @pl.when(r < NPIV)
+    def _():
+        child_part = z_ref.at[spot, pl.ds(0, 24)]
+        front_part = z_ref.at[spot, pl.ds(24, 6)]
+        pltpu.make_async_copy(child_part, child_part, got.at[0]).wait()
+        pltpu.make_async_copy(front_part, front_part, got.at[1]).wait()
+        for d in (4, 3, 5, 2, 6, 1, 7):
+            z_copy(d).start()
+
+    pltpu.make_async_copy(maps_ref, maps_ref, got.at[2]).wait()
+    for i in range(NPIV):
+        @pl.when(r != i)
+        def _():
+            pltpu.make_async_copy(z_ref.at[i], z_ref.at[i], z_got.at[i]).wait()
+
+    for t, (i, j) in enumerate(TILES):
+        acc_ref[t] = z_ref[i, 24 + j]
+
+    def add_child(q, carry):
+        wanted = maps_ref[q][:NPIV]
+        tiles = z_ref[:, pl.ds(q * 6, 6)]
+        for j in range(NPIV):
+            pick = jnp.where(wanted == float(j), 1.0, 0.0)[None, :, None, :]
+            strip = jnp.sum(tiles * pick, axis=1)
+            for i in range(j, NPIV):
+                pick = jnp.where(wanted == float(i), 1.0, 0.0)[:, None, :]
+                acc_ref[i * (i + 1) // 2 + j] += jnp.sum(strip * pick, axis=0)
+        return carry
+
+    lax.fori_loop(0, 4, add_child, 0)
+
+    own_k = pltpu.make_async_copy(acc_ref, k_ref.at[:, e], got.at[3])
+    own_k.start()
+
+    def k_copy(d):
+        return push(acc_ref, k_ref.at[:, e], send.at[4], k_got.at[d], chip_peer(d)[1])
+
+    def pair_copy(d):
+        spot_e = chip_peer(16 - d)[0]
+        return push(k_ref.at[:, spot_e], k_ref.at[:, spot_e], send.at[5], p_got.at[d], partner)
+
+    for d in range(1, 16):
+        k_copy(d).start()
+    own_k.wait()
+    pair_copy(0).start()
+
+    def forward(d, carry):
+        k_copy(d).wait_recv()
+        pair_copy(d).start()
+        return carry
+
+    lax.fori_loop(1, 16, forward, 0)
+
+    def finish(d, carry):
+        pair_copy(d).wait()
+        return carry
+
+    lax.fori_loop(0, 16, finish, 0)
+
+    def sent(d, carry):
+        k_copy(d).wait_send()
+        return carry
+
+    lax.fori_loop(1, 16, sent, 0)
+
+    @pl.when(has_child)
+    def _():
+        lax.fori_loop(1, 32, lambda d, carry: (child_copy(d).wait_send(), carry)[1], 0)
+
+    @pl.when(has_front)
+    def _():
+        lax.fori_loop(1, 32, lambda d, carry: (front_copy(d).wait_send(), carry)[1], 0)
+
+    for d in range(1, 4):
+        map_copy(d).wait_send()
+
+    @pl.when(r < NPIV)
+    def _():
+        for d in range(1, 8):
+            z_copy(d).wait_send()
+
+
+def gather_pivot(child, front, child_map):
+    return pl.pallas_call(
+        pivot_kernel,
+        out_shape=(
+            jax.ShapeDtypeStruct((NT_, 32, 4, BLK), jnp.float32),
+            jax.ShapeDtypeStruct((4, 16, BLK), jnp.float32),
+        ),
+        in_specs=[VM] * 3,
+        out_specs=(VM, VM),
+        scratch_shapes=[
+            pltpu.VMEM((NPIV, 30, 4, BLK), jnp.float32),
+            pltpu.VMEM((NT_, 4, BLK), jnp.float32),
+            pltpu.SemaphoreType.DMA((6,)),
+            pltpu.SemaphoreType.DMA((4,)),
+            pltpu.SemaphoreType.DMA((NPIV,)),
+            pltpu.SemaphoreType.DMA((16,)),
+            pltpu.SemaphoreType.DMA((16,)),
+        ],
+        compiler_params=pltpu.CompilerParams(collective_id=0, has_side_effects=True),
+        cost_estimate=pl.CostEstimate(flops=20_000_000_000, bytes_accessed=60_000_000, transcendentals=0),
+        name="gather_pivot",
+    )(child, front, child_map)
 
 
 def split(x):
@@ -220,53 +415,18 @@
     )(maps, where, buf)
 
 
-def place_pivot_kernel(map_ref, buf_ref, acc_ref):
-    for i in range(NPIV):
-        for j in range(NPIV):
-            acc_ref[i, j] = buf_ref[i, 32 + j]
-
-    def child_row(step, carry):
-        q = step // NPIV
-        block_row = step % NPIV
-        i = map_ref[q, block_row]
-
-        @pl.when(i < NPIV)
-        def _():
-            for block_col in range(NPIV):
-                j = map_ref[q, block_col]
-
-                @pl.when(j < NPIV)
-                def _():
-                    acc_ref[i, j] += buf_ref[block_row, block_col * 4 + q]
-
-        return carry
-
-    lax.fori_loop(0, 4 * NPIV, child_row, 0)
-
-
-def place_pivot(maps, buf):
-    return pl.pallas_call(
-        place_pivot_kernel,
-        out_shape=jax.ShapeDtypeStruct((NPIV, NPIV, 4, BLK), jnp.float32),
-        in_specs=[SM, VM],
-        out_specs=VM,
-        name="place_pivot",
-    )(maps, buf)
-
-
 def body(front, child, child_map):
+    child = child[0]
     where = jnp.stack([lax.axis_index(a) for a in ("row", "col", "sub")]).astype(jnp.int32)
-    maps = lax.all_gather(child_map[0], "sub")
+    wide = jnp.broadcast_to(child_map[0].astype(jnp.float32)[:, None], (16, BLK))
+    k, maps = gather_pivot(child[:BLK, :BLK].reshape(32, 4, BLK), front[:BLK, :BLK].reshape(32, 4, BLK), wide)
+    low, inv = factor(k.reshape(NT_, BLK, BLK))
+    maps = maps[:, :, 0].astype(jnp.int32)
     shares = child.reshape(2, 32, 4, 2, BLK).transpose(1, 0, 3, 2, 4)
     shares = lax.all_to_all(shares, PLANE, 0, 0, tiled=True)
     panel = front[:, :BLK].reshape(8, 32, 4, BLK).transpose(1, 0, 2, 3)
     panel = lax.all_to_all(panel, PLANE, 0, 0, tiled=True)
     panel = panel.reshape(8, 4, 8, 4, BLK)[:NPIV, 0]
-    pivot = jnp.concatenate([shares[:, 0, 0], panel[:, 0]], axis=0)
-    pivot = place_pivot(maps, lax.all_gather(pivot, "row"))
-    k = lax.all_gather(pivot, PLANE).transpose(1, 0, 3, 2, 4).reshape(PIV, PIV)
-    shares, _ = lax.optimization_barrier((shares, pivot))
-    low, inv = factor(k)
     buf = lax.all_gather(shares, "row").reshape(8, 8, 4, 2, 2, 4, BLK)
     acc = place(maps, where, buf)
     panel = panel + acc[:NPIV, 0, :, 0]

time: 289 us -> 222 us (0.77)
  waiting for transfers between devices: 82.1 us -> 0.05 us
  Pallas kernels: 91.3 us -> 132 us
  starting transfers between devices: 12.9 us -> 0.09 us
  blocking collectives: 65 us -> 52.9 us
  local copies, waits for them, and re-layouts: 20.7 us -> 17.5 us
    pallas_call x1, Pallas kernels: 2.94 us -> 44.7 us  [gather_pivot(): pl.pallas_call(pivot_kernel, out_shape=(jax.ShapeDtypeStruct((NT_, 32, 4,...]
    all_gather x2 -> x0, blocking collectives: 41.2 us -> none  [the longest x1 31.3 us: body(): pivot = place_pivot(maps, lax.all_gather(pivot, 'row'))]
    all_gather x1, waiting for transfers between devices: 38.6 us -> 0.01 us  [body(): buf = lax.all_gather(shares, 'row').reshape(8, 8, 4, 2, 2, 4, BLK)]
    all_to_all x0 -> x2, blocking collectives: none -> 30.7 us  [the longest x1 15.4 us: body(): panel = lax.all_to_all(panel, PLANE, 0, 0, tiled=True)]
    all_gather x1 -> x0, waiting for transfers between devices: 19.7 us -> none  [body(): k = lax.all_gather(pivot, PLANE).transpose(1, 0, 3, 2, 4).reshape(PIV, PIV)]
    all_gather x1, waiting for transfers between devices: 16.8 us -> 0.01 us  [body(): rows = lax.all_gather(panel, PLANE)]
    all_to_all x2 -> x0, starting transfers between devices: 12.7 us -> none  [the longest x1 7.62 us: body(): shares = lax.all_to_all(shares, PLANE, 0, 0, tiled=True)]
    all_to_all x2 -> x0, waiting for transfers between devices: 6.3 us -> none  [the longest x1 5.85 us: body(): shares = lax.all_to_all(shares, PLANE, 0, 0, tiled=True)]
  transfers between devices with their start and end apart: 6 -> 3, of which waited for: 5 -> 0; matrix products, arithmetic and copies ran while one was open for 5% -> 5% of each run, Pallas kernels for 26% -> 51%
where the time goes in v3:
time: 222 us; the launch traced here: 220 us
  Pallas kernels  132 us (59%)
  blocking collectives  52.9 us (24%)
  local copies, waits for them, and re-layouts  17.5 us (8%)
  between operations  13.2 us (6%)
  other arithmetic  3.85 us (2%)
    pallas_call x1, Pallas kernels, factor(): pl.pallas_call(factor_kernel, out_shape=(jax.ShapeDtypeStruct((PIV, PIV),...  67.7 us
    pallas_call x1, Pallas kernels, gather_pivot(): pl.pallas_call(pivot_kernel, out_shape=(jax.ShapeDtypeStruct((NT_, 32, 4,...  44.7 us
    all_to_all x1, blocking collectives, body(): lax.all_to_all(acc.reshape(32, 8, 2, 4, BLK), PLANE, 0, 0, tiled=True)  22.2 us
    all_to_all x1, blocking collectives, body(): panel = lax.all_to_all(panel, PLANE, 0, 0, tiled=True)  15.4 us
    all_to_all x1, blocking collectives, body(): shares = lax.all_to_all(shares, PLANE, 0, 0, tiled=True)  15.3 us
    pallas_call x1, Pallas kernels, schur(): pl.pallas_call(schur_kernel, out_shape=jax.ShapeDtypeStruct((1024, 256),...  13.5 us
    pallas_call x1, Pallas kernels, place(): pl.pallas_call(place_kernel, out_shape=jax.ShapeDtypeStruct((8, 4, 8, 2,...  6.25 us
  transfers between devices with their start and end apart: 3, of which 0 were waited for; matrix products, arithmetic and copies ran while one was open for 5% of the time, Pallas kernels for 51%

profile of v3, /device:TPU:2, one launch (start us, length us, event | category | flops | bytes accessed | tf_op | source)
XLA Modules:
  0.0 219.7 jit_solution(3385691486027488768)
XLA Ops:
  6.5 1.1 reshape_squeeze.3
  7.6 15.3 %all_to_all.15 = f32[32,2,2,4,128]{4,2,3,1,0:T(2,128)S(1)} all-to-all(f32[32,2,2,4,128]{4,2,3,1,0:T(2,128)S(1)} %copy.34), channel_id=1, replica_groups=mesh['row'=8,'col'=8,'sub'=4] {'col','sub'}, dimensions={0} | all-to-all | bytes 524288 | tf_op jit(solution)/shard_map/all_to_all | solution.py:426
  22.9 0.8 copy.35
  23.8 1.5 slice.34
  25.3 1.5 slice.27
  26.7 0.6 pad_add_fusion.where_ref
  27.4 0.7 convert_bitcast_fusion
  28.0 0.7 broadcast_in_dim.2.map_ref
  28.7 44.7 %gather_pivot.1 = (f32[21,32,4,128]{3,2,1,0:T(4,128)}, f32[4,16,128]{2,1,0:T(8,128)}) custom-call(f32[32,4,128]{2,1,0:T(4,128)} %bitcast.48, f32[32,4,128]{2,1,0:T(4,128)} %bitcast.49, f32[16,128]{1,0:T(8,128)} %broadcast_in_dim.2.map_ref), custom_call_target="tpu_custom_call" | custom-call | flops 20000000000 | bytes 60000000 | tf_op jit(solution)/shard_map/gather_pivot/pallas_call | solution.py:262
  73.4 1.5 convert_reduce_fusion.map_ref
  74.9 6.3 %place.1 = f32[8,4,8,2,4,128]{5,4,3,2,1,0:T(4,128)} custom-call(s32[4,16]{1,0:T(4,128)} %convert_reduce_fusion.map_ref, s32[3]{0:T(128)} %pad_add_fusion.where_ref, f32[8,8,4,2,2,4,128]{6,5,4,3,2,1,0:T(4,128)} %bitcast.44), custom_call_target="tpu_custom_call" | custom-call | tf_op jit(solution)/shard_map/place/pallas_call | solution.py:409
  81.1 1.9 copy.38
  83.0 22.2 %all_to_all.16 = f32[32,8,2,4,128]{4,2,3,1,0:T(2,128)S(1)} all-to-all(f32[32,8,2,4,128]{4,2,3,1,0:T(2,128)S(1)} %copy.38), channel_id=1, replica_groups=mesh['row'=8,'col'=8,'sub'=4] {'col','sub'}, dimensions={0} | all-to-all | bytes 2097152 | tf_op jit(solution)/shard_map/all_to_all | solution.py:435
  105.2 0.4 copy.39
  105.6 0.1 bitcast_add_fusion.matrix_ref
  105.7 0.7 slice.36
  106.7 15.4 %all_to_all.17 = f32[32,8,4,128]{3,2,1,0:T(4,128)S(1)} all-to-all(f32[32,8,4,128]{3,2,1,0:T(4,128)S(1)} %copy.31), channel_id=1, replica_groups=mesh['row'=8,'col'=8,'sub'=4] {'col','sub'}, dimensions={0} | all-to-all | bytes 1048576 | tf_op jit(solution)/shard_map/all_to_all | solution.py:428
  122.0 0.9 fusion
  123.0 0.6 copy.36
  123.6 67.7 %factor.1 = (f32[768,768]{1,0:T(8,128)}, f32[6,128,128]{2,1,0:T(8,128)}) custom-call(f32[21,128,128]{2,1,0:T(8,128)} %bitcast.50), custom_call_target="tpu_custom_call" | custom-call | flops 60000002048 | bytes 200000000 | tf_op jit(solution)/shard_map/factor/pallas_call | solution.py:81
  191.4 2.1 slice.37.top_ref
  193.5 3.8 %copy.37 = f32[8,32,4,6,128]{4,3,2,1,0:T(8,128)S(1)} copy(f32[8,32,4,6,128]{4,0,2,3,1:T(8,128)} %bitcast.42) | data formatting | bytes 6291456 | tf_op jit(solution)/shard_map/transpose | solution.py:434
  197.2 2.4 %copy.47 = f32[128,8,6,128]{3,1,2,0:T(8,128)} copy(f32[128,8,6,128]{3,2,1,0:T(8,128)S(1)} %bitcast.37) | data formatting | bytes 6291456
  199.6 13.5 %schur.1 = f32[1024,256]{1,0:T(8,128)} custom-call(s32[3]{0:T(128)} %pad_add_fusion.where_ref, f32[1024,768]{1,0:T(8,128)} %bitcast.38, f32[768,256]{1,0:T(8,128)} %slice.37.top_ref, f32[1024,256]{1,0:T(8,128)} %copy-done, f32[768,768]{1,0:T(8,128)} %get-tuple-element.11.low_ref, f32[6,128,128]{2,1,0:T(8,128)} %get-tuple-element.12.inv_ref), custom_call_target="tpu_custom_call" | custom-call | tf_op jit(solution)/shard_map/schur/pallas_call | solution.py:360
  (17 shorter events, 0.3 us)
Async XLA Ops:
  6.5 68.3 %all-gather.8.cloned.1.call-start = ((), (), s32[]{:S(2)}) async-start(), calls=%async_computation.4 | async-start | bytes 2359296 | tf_op jit(solution)/shard_map/all_gather | solution.py:430
  23.7 167.6 %all-gather.10.cloned.1.call-start = ((), (), s32[]{:S(2)}) async-start(), calls=%async_computation.5 | async-start | bytes 1179648 | tf_op jit(solution)/shard_map/all_gather | solution.py:437
  81.1 24.4 %copy-start.1 = (f32[1024,256]{1,0:T(8,128)S(1)}, f32[1024,256]{1,0:T(8,128)}, u32[]{:S(2)}) copy-start(f32[1024,256]{1,0:T(8,128)} %param.3) | copy-start | bytes 3145732
  105.2 1.4 slice-start
  105.7 85.7 %copy-start = (f32[1024,256]{1,0:T(8,128)}, f32[1024,256]{1,0:T(8,128)S(1)}, u32[]{:S(2)}) copy-start(f32[1024,256]{1,0:T(8,128)S(1)} %bitcast_add_fusion.matrix_ref) | copy-start | bytes 3145732
  106.5 87.0 %all-gather.6.cloned.1.call-start = ((), (), s32[]{:S(2)}) async-start(), calls=%async_computation.3 | async-start | bytes 3244032 | tf_op jit(solution)/shard_map/all_gather | solution.py:433
Sparse Core Ops, SparseCore 0:
  23.9 50.6 all-gather.7
  106.6 35.7 all-gather.9
  144.9 48.0 all-gather.5

commit v4 on v2

v4 whole, which is shorter than its diff:
```python
import jax
import jax.numpy as jnp
from jax import lax
from jax.experimental import pallas as pl
from jax.experimental.pallas import tpu as pltpu
from jax.sharding import PartitionSpec as P

BLK = 128
NPIV = 6
PIV = NPIV * BLK
PLANE = ("col", "sub")
HI = lax.Precision.HIGHEST
VM = pl.BlockSpec(memory_space=pltpu.VMEM)
SM = pl.BlockSpec(memory_space=pltpu.SMEM)


def nt(a, b, precision=HI):
    return lax.dot_general(a, b, (((1,), (1,)), ((), ())), precision=precision, preferred_element_type=jnp.float32)
def tn(a, b, precision=HI):
    return lax.dot_general(a, b, (((0,), (0,)), ((), ())), precision=precision, preferred_element_type=jnp.float32)

def rsqrt(x):
    return lax.rsqrt(x)

def eliminate(a_ref):
    sub = lax.broadcasted_iota(jnp.int32, (8, 256), 0)
    for g in range(16):
        rows = a_ref[8 * g : 8 * g + 8, :]
        left = rows[:, :BLK]
        e = {}
        for j in range(8):
            c = jnp.broadcast_to(left[:, 8 * g + j : 8 * g + j + 1], (8, BLK))
            for i in range(j, 8):
                e[j, i] = jnp.broadcast_to(c[i : i + 1, :], (8, BLK))
        r = [jnp.broadcast_to(rows[i : i + 1, :], (8, 256)) for i in range(8)]
        out = None
        for j in range(8):
            s = rsqrt(e[j, j])
            u = {i: e[j, i] * s for i in range(j + 1, 8)}
            for i in range(j + 1, 8):
                for m in range(i, 8):
                    e[i, m] = e[i, m] - u[i] * u[m]
            rj = r[j] * jnp.concatenate([s, s], axis=1)
            for i in range(j + 1, 8):
                r[i] = r[i] - jnp.concatenate([u[i], u[i]], axis=1) * rj
            out = rj if out is None else jnp.where(sub == j, rj, out)
        a_ref[8 * g : 8 * g + 8, :] = out
        if g < 15:
            t = tn(out[:, :BLK], out)
            a_ref[8 * g + 8 :, :] = a_ref[8 * g + 8 :, :] - t[8 * g + 8 :, :]

def factor_steps(k_ref, l_ref, y_ref, a_ref, m_ref, progress):
    r_iota = lax.broadcasted_iota(jnp.int32, (BLK, BLK), 0)
    c_iota = lax.broadcasted_iota(jnp.int32, (BLK, BLK), 1)
    for i in range(NPIV):
        for j in range(i + 1):
            m_ref[i * BLK : (i + 1) * BLK, j * BLK : (j + 1) * BLK] = k_ref[i * (i + 1) // 2 + j]
        if i < NPIV - 1:
            m_ref[i * BLK : (i + 1) * BLK, (i + 1) * BLK :] = jnp.zeros((BLK, PIV - (i + 1) * BLK), jnp.float32)
    l_ref[...] = jnp.zeros_like(l_ref)

    def step(b, carry):
        progress(b)
        at = pl.ds(pl.multiple_of(b * BLK, BLK), BLK)
        a_ref[:, :BLK] = m_ref[at, at]
        a_ref[:, BLK:] = jnp.where(r_iota == c_iota, 1.0, 0.0)
        eliminate(a_ref)
        y = a_ref[:, BLK:]
        y_ref[b] = y
        l_ref[at, at] = jnp.where(r_iota >= c_iota, a_ref[:, :BLK].T, 0.0)

        def solve(i, c):
            rows = pl.ds(pl.multiple_of(i * BLK, BLK), BLK)
            l_ref[rows, at] = nt(m_ref[rows, at], y)
            return c

        lax.fori_loop(b + 1, NPIV, solve, 0)

        def update(i, c):
            rows = pl.ds(pl.multiple_of(i * BLK, BLK), BLK)
            m_ref[rows, :] = m_ref[rows, :] - nt(l_ref[rows, at], l_ref[:, at])
            return c

        lax.fori_loop(b + 1, NPIV, update, 0)
        return carry

    lax.fori_loop(0, NPIV, step, 0)


MESH = pl.DeviceIdType.MESH
TILES = [(i, j) for i in range(NPIV) for j in range(i + 1)]
NTILE = len(TILES)


class Place:
    def __init__(self):
        self.r, self.c, self.s = (lax.axis_index(a) for a in ("row", "col", "sub"))
        self.e = self.c * 4 + self.s
        self.core = self.c % 2
        self.chip = (self.c // 2) * 4 + self.s
        self.partner = (self.r, self.c + 1 - 2 * self.core, self.s)

    def plane(self, d):
        p = (self.e + d) % 32
        return p, (self.r, p // 4, p % 4)

    def same_core(self, d):
        p = (self.chip + d) % 16
        c = (p // 4) * 2 + self.core
        return c * 4 + p % 4, (self.r, c, p % 4)

    def line(self, d):
        return ((self.r + d) % 8, self.c, self.s)

    def greet(self):
        barrier = pltpu.get_barrier_semaphore()

        def plane(d, carry):
            pl.semaphore_signal(barrier, inc=1, device_id=self.plane(d)[1], device_id_type=MESH)
            return carry

        def line(d, carry):
            pl.semaphore_signal(barrier, inc=1, device_id=self.line(d), device_id_type=MESH)
            return carry

        lax.fori_loop(1, 32, plane, 0)
        lax.fori_loop(1, 8, line, 0)
        pl.semaphore_wait(barrier, 38)


def push(src, dst, ssem, rsem, device):
    return pltpu.make_async_remote_copy(
        src_ref=src, dst_ref=dst, send_sem=ssem, recv_sem=rsem, device_id=device, device_id_type=MESH
    )


def arrive(ref, sem):
    pltpu.make_async_copy(ref, ref, sem).wait()


def loop(low, high, f):
    def one(d, carry):
        f(d)
        return carry

    lax.fori_loop(low, high, one, 0)


def gather_kernel(
    child_ref, front_ref, map_ref, k_ref, maps_ref, buf_ref, panel_ref,
    z_ref, acc_ref, send, got, z_got, f_got, k_got, p_got, right_got, left_got,
):
    at = Place()
    r, c, s, e = at.r, at.c, at.s, at.e
    at.greet()
    pivot_row = r < NPIV
    has_front = (c < NPIV) & (s == 0)
    spot = jnp.minimum(r, NPIV - 1)
    seat = jnp.minimum(c, NPIV - 1)

    def child_copy(d):
        p, device = at.plane(d)
        return push(child_ref.at[:, :, p], buf_ref.at[r, e], send.at[0], got.at[0], device)

    def front_copy(d):
        p, device = at.plane(d)
        return push(front_ref.at[:, p], panel_ref.at[seat], send.at[1], got.at[1], device)

    def map_copy(d):
        return push(map_ref, maps_ref.at[s], send.at[2], got.at[2], (r, c, (s + d) % 4))

    pltpu.make_async_copy(child_ref.at[:, :, e], buf_ref.at[r, e], got.at[0]).start()
    pltpu.make_async_copy(map_ref, maps_ref.at[s], got.at[2]).start()
    loop(1, 32, lambda d: child_copy(d).start())

    @pl.when(has_front)
    def _():
        pltpu.make_async_copy(front_ref.at[:, e], panel_ref.at[seat], got.at[1]).start()
        loop(1, 32, lambda d: front_copy(d).start())

    for d in range(1, 4):
        map_copy(d).start()

    def z_copy(d):
        return push(buf_ref.at[spot, pl.ds(0, 24), 0, 0], z_ref.at[spot, pl.ds(0, 24)], send.at[3], z_got.at[spot], at.line(d))

    def f_copy(d):
        return push(panel_ref.at[:, 0], z_ref.at[spot, pl.ds(24, 6)], send.at[4], f_got.at[spot], at.line(d))

    def right_copy(k):
        block = (r + 8 - k) % 8
        return push(buf_ref.at[block], buf_ref.at[block], send.at[5], right_got.at[k], at.line(1))

    def left_copy(k):
        block = (r + k) % 8
        return push(buf_ref.at[block], buf_ref.at[block], send.at[6], left_got.at[k], at.line(7))

    def right_wait(k):
        arrive(buf_ref.at[(r + 7 - k) % 8], right_got.at[k])

    def left_wait(k):
        arrive(buf_ref.at[(r + 1 + k) % 8], left_got.at[k])

    arrive(buf_ref.at[r], got.at[0])
    arrive(panel_ref, got.at[1])

    @pl.when(pivot_row)
    def _():
        pltpu.make_async_copy(buf_ref.at[spot, pl.ds(0, 24), 0, 0], z_ref.at[spot, pl.ds(0, 24)], z_got.at[spot]).start()
        pltpu.make_async_copy(panel_ref.at[:, 0], z_ref.at[spot, pl.ds(24, 6)], f_got.at[spot]).start()
        for d in (4, 3, 5, 2, 6, 1, 7):
            z_copy(d).start()
            f_copy(d).start()

    right_copy(0).start()
    left_copy(0).start()
    arrive(maps_ref, got.at[2])
    for i in range(NPIV):
        arrive(z_ref.at[i, pl.ds(0, 24)], z_got.at[i])
        arrive(z_ref.at[i, pl.ds(24, 6)], f_got.at[i])

    for t, (i, j) in enumerate(TILES):
        acc_ref[t] = z_ref[i, 24 + j]

    def add_child(q):
        wanted = maps_ref[q][:NPIV]
        strips = []
        for j in range(NPIV):
            strip = None
            for seat_j in range(j + 1):
                pick = jnp.where(wanted[seat_j : seat_j + 1] == float(j), 1.0, 0.0)[None]
                term = z_ref[:, seat_j * 4 + q] * pick
                strip = term if strip is None else strip + term
            strips.append(strip)
        for j in range(NPIV):
            for i in range(j, NPIV):
                pick = jnp.where(wanted == float(i), 1.0, 0.0)[:, None, :]
                acc_ref[i * (i + 1) // 2 + j] += jnp.sum(strips[j] * pick, axis=0)

    loop(0, 4, add_child)

    own_k = pltpu.make_async_copy(acc_ref, k_ref.at[:, e], got.at[3])
    own_k.start()

    def k_copy(d):
        return push(acc_ref, k_ref.at[:, e], send.at[7], k_got.at[d], at.same_core(d)[1])

    def pair_copy(d):
        where_e = at.same_core(16 - d)[0]
        return push(k_ref.at[:, where_e], k_ref.at[:, where_e], send.at[8], p_got.at[d], at.partner)

    def forward(d):
        k_copy(d).wait_recv()
        pair_copy(d).start()

    loop(1, 16, lambda d: k_copy(d).start())
    right_wait(0)
    right_copy(1).start()
    left_wait(0)
    left_copy(1).start()
    own_k.wait()
    pair_copy(0).start()
    right_wait(1)
    right_copy(2).start()
    left_wait(1)
    left_copy(2).start()
    loop(1, 16, forward)
    right_wait(2)
    right_copy(3).start()
    left_wait(2)
    loop(0, 16, lambda d: pair_copy(d).wait())
    right_wait(3)

    loop(1, 16, lambda d: k_copy(d).wait_send())
    loop(1, 32, lambda d: child_copy(d).wait_send())

    @pl.when(has_front)
    def _():
        loop(1, 32, lambda d: front_copy(d).wait_send())

    for d in range(1, 4):
        map_copy(d).wait_send()

    @pl.when(pivot_row)
    def _():
        for d in range(1, 8):
            z_copy(d).wait_send()
            f_copy(d).wait_send()

    for k in range(4):
        right_copy(k).wait_send()
    for k in range(3):
        left_copy(k).wait_send()


def gather_all(child, front, child_map):
    dma = pltpu.SemaphoreType.DMA
    return pl.pallas_call(
        gather_kernel,
        out_shape=(
            jax.ShapeDtypeStruct((NTILE, 32, 4, BLK), jnp.float32),
            jax.ShapeDtypeStruct((4, 16, BLK), jnp.float32),
            jax.ShapeDtypeStruct((8, 32, 2, 2, 4, BLK), jnp.float32),
            jax.ShapeDtypeStruct((NPIV, 8, 4, BLK), jnp.float32),
        ),
        in_specs=[VM] * 3,
        out_specs=(VM,) * 4,
        scratch_shapes=[
            pltpu.VMEM((NPIV, 30, 4, BLK), jnp.float32),
            pltpu.VMEM((NTILE, 4, BLK), jnp.float32),
            dma((9,)), dma((4,)), dma((NPIV,)), dma((NPIV,)), dma((16,)), dma((16,)), dma((4,)), dma((3,)),
        ],
        compiler_params=pltpu.CompilerParams(collective_id=0, has_side_effects=True),
        name="gather_all",
    )(child, front, child_map)


def factor_kernel(
    k_ref, acc_ref, panel_ref, front_ref, low_ref, inv_ref, rows_ref, moved_ref, top_ref,
    a_ref, m_ref, share_ref, w_ref, send, got, r_got, p_got, t_got,
):
    at = Place()
    r, c, s, e = at.r, at.c, at.s, at.e
    at.greet()
    spot = jnp.minimum(r, NPIV - 1)

    def move_copy(d):
        p, device = at.plane(d)
        return push(acc_ref.at[p], moved_ref.at[:, :, e], send.at[0], got.at[0], device)

    pltpu.make_async_copy(acc_ref.at[e], moved_ref.at[:, :, e], got.at[0]).start()
    loop(1, 32, lambda d: move_copy(d).start())

    for j in range(NPIV):
        for slot in range(8):
            share_ref[slot, j] = acc_ref[j * 4, slot, 0] + panel_ref[j, slot]

    own_rows = pltpu.make_async_copy(share_ref, rows_ref.at[:, :, e], got.at[1])

    def rows_copy(d):
        return push(share_ref, rows_ref.at[:, :, e], send.at[1], r_got.at[d], at.same_core(d)[1])

    def pair_copy(d):
        where_e = at.same_core(16 - d)[0]
        return push(rows_ref.at[:, :, where_e], rows_ref.at[:, :, where_e], send.at[2], p_got.at[d], at.partner)

    def top_copy(d):
        return push(w_ref, top_ref.at[spot], send.at[3], t_got.at[spot], at.line(d))

    own_rows.start()
    loop(1, 16, lambda d: rows_copy(d).start())

    def after_first():
        own_rows.wait()
        pair_copy(0).start()
        arrive(moved_ref, got.at[0])

        @pl.when(r < NPIV)
        def _():
            w_ref[...] = moved_ref[0] + front_ref[...]
            pltpu.make_async_copy(w_ref, top_ref.at[spot], t_got.at[spot]).start()
            for d in (4, 3, 5, 2, 6, 1, 7):
                top_copy(d).start()

    def forward(d):
        rows_copy(d).wait_recv()
        pair_copy(d).start()

    def progress(b):
        pl.when(b == 1)(after_first)
        pl.when(b == 3)(lambda: loop(1, 16, forward))

    factor_steps(k_ref, low_ref, inv_ref, a_ref, m_ref, progress)

    loop(0, 16, lambda d: pair_copy(d).wait())
    for i in range(NPIV):
        arrive(top_ref.at[i], t_got.at[i])
    loop(1, 16, lambda d: rows_copy(d).wait_send())
    loop(1, 32, lambda d: move_copy(d).wait_send())

    @pl.when(r < NPIV)
    def _():
        for d in range(1, 8):
            top_copy(d).wait_send()


def factor_all(k, acc, panel, front):
    dma = pltpu.SemaphoreType.DMA
    f32 = lambda *shape: jax.ShapeDtypeStruct(shape, jnp.float32)
    return pl.pallas_call(
        factor_kernel,
        out_shape=(
            f32(PIV, PIV),
            f32(NPIV, BLK, BLK),
            f32(8, NPIV, 32, 4, BLK),
            f32(8, 2, 32, 4, BLK),
            f32(NPIV, 2, 32, 4, BLK),
        ),
        in_specs=[VM] * 4,
        out_specs=(VM,) * 5,
        scratch_shapes=[
            pltpu.VMEM((BLK, 256), jnp.float32),
            pltpu.VMEM((PIV, PIV), jnp.float32),
            pltpu.VMEM((8, NPIV, 4, BLK), jnp.float32),
            pltpu.VMEM((2, 32, 4, BLK), jnp.float32),
            dma((4,)), dma((2,)), dma((16,)), dma((16,)), dma((NPIV,)),
        ],
        compiler_params=pltpu.CompilerParams(collective_id=1, has_side_effects=True, vmem_limit_bytes=40 * 1024 * 1024),
        name="factor_all",
    )(k, acc, panel, front)


def place_kernel(map_ref, where_ref, buf_ref, acc_ref):
    acc_ref[...] = jnp.zeros_like(acc_ref)
    row = where_ref[0]

    def child_row(step):
        q = step // 16
        block_row = step % 16
        i = map_ref[q, block_row]

        @pl.when(i % 8 == row)
        def _():
            slot = i // 8
            for block_col in range(16):
                j = map_ref[q, block_col]
                tile = buf_ref[block_row % 8, block_col % 8 * 4 + q, block_row // 8, block_col // 8]
                acc_ref[j % 8 * 4 + j // 16, slot, (j // 8) % 2] += tile

    loop(0, 64, child_row)


def place(maps, where, buf):
    return pl.pallas_call(
        place_kernel,
        out_shape=jax.ShapeDtypeStruct((32, 8, 2, 4, BLK), jnp.float32),
        in_specs=[SM, SM, VM],
        out_specs=VM,
        name="place",
    )(maps, where, buf)


def split(x):
    high = x.astype(jnp.bfloat16)
    return high, (x - high.astype(jnp.float32)).astype(jnp.bfloat16)


def dot3(a, b, dims):
    def one(x, y):
        return lax.dot_general(x, y, (dims, ((), ())), preferred_element_type=jnp.float32)

    return one(a[0], b[0]) + (one(a[0], b[1]) + one(a[1], b[0]))


NT = ((1,), (1,))
NN = ((1,), (0,))


def schur_kernel(
    where_ref, rows_ref, top_ref, moved_ref, front_ref, low_ref, inv_ref, out_ref,
    lh, ll, yh, yl, uh, ul, x_ref,
):
    tile = pl.program_id(0)
    row, col, sub = where_ref[0], where_ref[1], where_ref[2]

    @pl.when(tile == 0)
    def _():
        high, rest = split(low_ref[...])
        lh[...] = high
        ll[...] = rest
        zero = jnp.zeros((BLK, BLK), jnp.float32)
        for p in range(3):
            first, second = inv_ref[2 * p], inv_ref[2 * p + 1]
            at = 256 * p
            cross = jnp.dot(low_ref[at + BLK : at + 256, at : at + BLK], first, precision=HI)
            cross = -jnp.dot(second, cross, precision=HI)
            pair = jnp.concatenate(
                [jnp.concatenate([first, zero], axis=1), jnp.concatenate([cross, second], axis=1)], axis=0
            )
            high, rest = split(pair)
            yh[p] = high
            yl[p] = rest
        for p in range(3):
            at = 256 * p
            x = four(top_ref[2 * p, 0], top_ref[2 * p, 1], top_ref[2 * p + 1, 0], top_ref[2 * p + 1, 1])
            if p:
                x = x - dot3((lh[at : at + 256, :at], ll[at : at + 256, :at]), (uh[:at, :], ul[:at, :]), NN)
            high, rest = split(dot3((yh[p], yl[p]), split(x), NN))
            uh[at : at + 256, :] = high
            ul[at : at + 256, :] = rest

    acc = front_ref[...] + four(moved_ref[0, 0], moved_ref[0, 1], moved_ref[1, 0], moved_ref[1, 1])
    xs = []
    for p in range(3):
        at = 256 * p
        x = four(rows_ref[0, 2 * p], rows_ref[0, 2 * p + 1], rows_ref[1, 2 * p], rows_ref[1, 2 * p + 1])
        for m in range(p):
            cut = slice(256 * m, 256 * m + 256)
            x = x - dot3(xs[m], (lh[at : at + 256, cut], ll[at : at + 256, cut]), NT)
        x = dot3(split(x), (yh[p], yl[p]), NT)
        x_ref[:, at : at + 256] = x
        xs.append(split(x))
        acc = acc - dot3(xs[p], (uh[at : at + 256, :], ul[at : at + 256, :]), NN)
    out_ref[...] = acc

    @pl.when((tile == 0) & (row < NPIV))
    def _():
        out_ref[:BLK, :] = jnp.zeros((BLK, 256), jnp.float32)
        x_ref[:BLK, :] = low_ref[pl.ds(pl.multiple_of(row * BLK, BLK), BLK), :]

    @pl.when((sub == 0) & (col < NPIV))
    def _():
        out_ref[:, :BLK] = x_ref[:, pl.ds(pl.multiple_of(col * BLK, BLK), BLK)]


def four(a, b, c, d):
    return jnp.concatenate([jnp.concatenate([a, b], axis=1), jnp.concatenate([c, d], axis=1)], axis=0)


def schur(where, rows, top, moved, front, low, inv):
    whole = lambda *shape: pl.BlockSpec(shape, lambda t: (0,) * len(shape), pipeline_mode=pl.Buffered(1))
    return pl.pallas_call(
        schur_kernel,
        out_shape=jax.ShapeDtypeStruct((1024, 256), jnp.float32),
        grid=(4,),
        in_specs=[
            SM,
            pl.BlockSpec((2, NPIV, BLK, BLK), lambda t: (t, 0, 0, 0)),
            whole(NPIV, 2, BLK, BLK),
            pl.BlockSpec((2, 2, BLK, BLK), lambda t: (t, 0, 0, 0)),
            pl.BlockSpec((256, 256), lambda t: (t, 0)),
            whole(PIV, PIV),
            whole(NPIV, BLK, BLK),
        ],
        out_specs=pl.BlockSpec((256, 256), lambda t: (t, 0)),
        scratch_shapes=[
            pltpu.VMEM((PIV, PIV), jnp.bfloat16),
            pltpu.VMEM((PIV, PIV), jnp.bfloat16),
            pltpu.VMEM((3, 256, 256), jnp.bfloat16),
            pltpu.VMEM((3, 256, 256), jnp.bfloat16),
            pltpu.VMEM((PIV, 256), jnp.bfloat16),
            pltpu.VMEM((PIV, 256), jnp.bfloat16),
            pltpu.VMEM((256, PIV), jnp.float32),
        ],
        name="schur",
    )(where, rows, top, moved, front, low, inv)


def body(front, child, child_map):
    where = jnp.stack([lax.axis_index(a) for a in ("row", "col", "sub")]).astype(jnp.int32)
    wide = jnp.broadcast_to(child_map[0].astype(jnp.float32)[:, None], (16, BLK))
    shares = child[0].reshape(2, BLK, 2, BLK).transpose(0, 2, 1, 3).reshape(2, 2, 32, 4, BLK)
    k, maps, buf, panel = gather_all(shares, front[:, :BLK].reshape(8, 32, 4, BLK), wide)
    acc = place(maps[:, :, 0].astype(jnp.int32), where, buf)
    first = front[:BLK].reshape(BLK, 2, BLK).transpose(1, 0, 2).reshape(2, 32, 4, BLK)
    low, inv, rows, moved, top = factor_all(k.reshape(NTILE, BLK, BLK), acc, panel, first)
    return schur(
        where,
        rows.reshape(8, NPIV, BLK, BLK),
        top.reshape(NPIV, 2, BLK, BLK),
        moved.reshape(8, 2, BLK, BLK),
        front,
        low,
        inv,
    )


def solution(mesh):
    placed = (P("row", ("col", "sub")), P("sub", "row", "col"), P("sub", None))
    return jax.shard_map(
        body, mesh=mesh, in_specs=placed, out_specs=P("row", ("col", "sub")), check_vma=False
    )
```

time: 289 us -> 187 us (0.65)
  waiting for transfers between devices: 82.1 us -> 0 us
  Pallas kernels: 91.3 us -> 173 us
  blocking collectives: 65 us -> 0 us
  between operations: 13.3 us -> 0.06 us
  starting transfers between devices: 12.9 us -> 0 us
  local copies, waits for them, and re-layouts: 20.7 us -> 12.2 us
    pallas_call x3, Pallas kernels: 77.8 us -> 159 us  [the longest x1 92.2 us: factor_all(): pl.pallas_call(factor_kernel, out_shape=(f32(PIV, PIV), f32(NPIV, BLK, BL...]
    all_gather x4 -> x0, waiting for transfers between devices: 75.1 us -> none  [the longest x1 38.6 us: body(): buf = lax.all_gather(shares, 'row').reshape(8, 8, 4, 2, 2, 4, BLK)]
    all_gather x2 -> x0, blocking collectives: 41.2 us -> none  [the longest x1 31.3 us: body(): pivot = place_pivot(maps, lax.all_gather(pivot, 'row'))]
    all_to_all x1 -> x0, blocking collectives: 23.8 us -> none  [body(): lax.all_to_all(acc.reshape(32, 8, 2, 4, BLK), PLANE, 0, 0, tiled=True)]
    all_to_all x2 -> x0, starting transfers between devices: 12.7 us -> none  [the longest x1 7.62 us: body(): shares = lax.all_to_all(shares, PLANE, 0, 0, tiled=True)]
    all_to_all x2 -> x0, waiting for transfers between devices: 6.3 us -> none  [the longest x1 5.85 us: body(): shares = lax.all_to_all(shares, PLANE, 0, 0, tiled=True)]
    transpose x4 -> x0, local copies, waits for them, and re-layouts: 5.81 us -> none  [the longest x1 3.78 us: body(): rows = rows.transpose(2, 0, 3, 1, 4).reshape(1024, PIV)]
    unnamed x8 -> x16, local copies, waits for them, and re-layouts: 4.35 us -> 6.94 us
  transfers between devices with their start and end apart: 6 -> 0, of which waited for: 5 -> 0; matrix products, arithmetic and copies ran while one was open for 5% -> 0% of each run, Pallas kernels for 26% -> 0%
where the time goes in v4:
time: 187 us; the launch traced here: 188 us
  Pallas kernels  173 us (93%)
  local copies, waits for them, and re-layouts  12.2 us (7%)
  other arithmetic  2.89 us (2%)
    pallas_call x1, Pallas kernels, factor_all(): pl.pallas_call(factor_kernel, out_shape=(f32(PIV, PIV), f32(NPIV, BLK, BL...  92.2 us
    pallas_call x1, Pallas kernels, gather_all(): pl.pallas_call(gather_kernel, out_shape=(jax.ShapeDtypeStruct((NTILE, 32,...  59.9 us
    pallas_call x1, Pallas kernels, schur(): pl.pallas_call(schur_kernel, out_shape=jax.ShapeDtypeStruct((1024, 256),...  13.7 us
    unnamed x16, local copies, waits for them, and re-layouts  6.94 us
    pallas_call x1, Pallas kernels, place(): pl.pallas_call(place_kernel, out_shape=jax.ShapeDtypeStruct((32, 8, 2, 4,...  6.71 us

profile of v4, /device:TPU:2, one launch (start us, length us, event | category | flops | bytes accessed | tf_op | source)
XLA Modules:
  0.0 187.7 jit_solution(6719786365288544714)
XLA Ops:
  0.0 0.6 pad_add_fusion.where_ref
  0.6 0.7 convert_bitcast_fusion
  1.3 0.7 broadcast_in_dim.2.map_ref
  2.0 0.9 copy_bitcast_fusion
  2.9 1.1 reshape_squeeze.3
  4.0 0.7 copy.6
  4.7 1.9 slice.9
  6.6 59.9 %gather_all.1 = (f32[21,32,4,128]{3,2,1,0:T(4,128)}, f32[4,16,128]{2,1,0:T(8,128)}, f32[8,32,2,2,4,128]{5,4,3,2,1,0:T(4,128)}, f32[6,8,4,128]{3,2,1,0:T(4,128)}) custom-call(f32[2,2,32,4,128]{4,3,2,1,0:T(4,128)} %bitcast.27, f32[8,32,4,128]{3,2,1,0:T(4,128)} %bitcast.26, f32[16,128]{1,0:T(8,128)} %broadcast_in_dim.2.map_ref), custom_call_target="tpu_custom_call" | custom-call | tf_op jit(solution)/shard_map/gather_all/pallas_call | solution.py:298
  66.4 0.0 copy-start.3
  66.4 0.0 copy-start.7
  66.5 1.6 convert_reduce_fusion.map_ref
  68.0 6.7 %place.1.acc_ref = f32[32,8,2,4,128]{4,3,2,1,0:T(4,128)} custom-call(s32[4,16]{1,0:T(4,128)} %convert_reduce_fusion.map_ref, s32[3]{0:T(128)} %pad_add_fusion.where_ref, f32[8,32,2,2,4,128]{5,4,3,2,1,0:T(4,128)} %get-tuple-element.16.buf_ref), custom_call_target="tpu_custom_call" | custom-call | tf_op jit(solution)/shard_map/place/pallas_call | solution.py:434
  74.8 0.0 copy-done.3
  74.8 0.0 copy-done.7
  74.8 0.0 copy-start
  74.8 1.2 copy-done
  76.0 92.2 %factor_all.1 = (f32[768,768]{1,0:T(8,128)S(1)}, f32[6,128,128]{2,1,0:T(8,128)S(1)}, f32[8,6,32,4,128]{4,3,2,1,0:T(4,128)S(1)}, f32[8,2,32,4,128]{4,3,2,1,0:T(4,128)S(1)}, f32[6,2,32,4,128]{4,3,2,1,0:T(4,128)S(1)}) custom-call(f32[21,128,128]{2,1,0:T(8,128)S(1)} %bitcast.22, f32[32,8,2,4,128]{4,3,2,1,0:T(4,128)S(1)} %copy-done, ...), custom_call_target="tpu_custom_call" | custom-call | tf_op jit(solution)/shard_map/factor_all/pallas_call | solution.py:390
  168.2 0.0 copy-start.1
  168.2 1.6 copy-done.1
  169.9 1.5 copy-done.2
  171.3 1.0 copy-done.4
  172.3 0.9 copy-done.5
  173.2 0.7 copy-done.6
  174.0 13.7 %schur.1 = f32[1024,256]{1,0:T(8,128)} custom-call(s32[3]{0:T(128)} %pad_add_fusion.where_ref, f32[8,6,128,128]{3,2,1,0:T(8,128)} %bitcast.21, f32[6,2,128,128]{3,2,1,0:T(8,128)} %bitcast.24, f32[8,2,128,128]{3,2,1,0:T(8,128)} %bitcast.23, f32[1024,256]{1,0:T(8,128)} %front_ref.1, f32[768,768]{1,0:T(8,128)} %copy-done.2, f32[6,128,128]{2,1,0:T(8,128)} %copy-done.6), custom_call_target="tpu_custom_call" | custom-call | tf_op jit(solution)/shard_map/schur/pallas_call | solution.py:522
  (4 shorter events, 0.0 us)
Async XLA Ops:
  66.4 8.3 %copy-start.3 = (f32[21,32,4,128]{3,2,1,0:T(4,128)S(1)}, f32[21,32,4,128]{3,2,1,0:T(4,128)}, u32[]{:S(2)}) copy-start(f32[21,32,4,128]{3,2,1,0:T(4,128)} %get-tuple-element.14) | copy-start | bytes 4128772
  66.4 8.3 %copy-start.7 = (f32[6,8,4,128]{3,2,1,0:T(4,128)S(1)}, f32[6,8,4,128]{3,2,1,0:T(4,128)}, u32[]{:S(2)}) copy-start(f32[6,8,4,128]{3,2,1,0:T(4,128)} %get-tuple-element.17.panel_ref) | copy-start | bytes 294916
  74.8 1.2 copy-start
  168.2 1.6 copy-start.1
  169.9 1.5 copy-start.2
  171.3 1.0 copy-start.4
  172.3 0.9 copy-start.5
  173.2 0.7 copy-start.6

commit v5 on v4

--- a/solution.py
+++ b/solution.py
@@ -19,13 +19,41 @@
 def tn(a, b, precision=HI):
     return lax.dot_general(a, b, (((0,), (0,)), ((), ())), precision=precision, preferred_element_type=jnp.float32)
 
+def split(x):
+    high = x.astype(jnp.bfloat16)
+    return high, (x - high.astype(jnp.float32)).astype(jnp.bfloat16)
+
+
+def dot3(a, b, dims):
+    def one(x, y):
+        return lax.dot_general(x, y, (dims, ((), ())), preferred_element_type=jnp.float32)
+
+    return one(a[0], b[0]) + (one(a[0], b[1]) + one(a[1], b[0]))
+
+
+def tn3(a, b):
+    return dot3(split(a), split(b), ((0,), (0,)))
+
+
+def nt3(a, b):
+    return dot3(split(a), split(b), ((1,), (1,)))
+
+
 def rsqrt(x):
     return lax.rsqrt(x)
 
+def wide(x):
+    return jnp.concatenate([x, x], axis=1)
+
 def eliminate(a_ref):
     sub = lax.broadcasted_iota(jnp.int32, (8, 256), 0)
+    ahead = []
     for g in range(16):
-        rows = a_ref[8 * g : 8 * g + 8, :]
+        if g == 0:
+            ahead = [a_ref[8 * h : 8 * h + 8, :] for h in range(2 + 1)]
+        elif g + 2 < 16:
+            ahead.append(a_ref[8 * (g + 2) : 8 * (g + 2) + 8, :])
+        rows = ahead.pop(0)
         left = rows[:, :BLK]
         e = {}
         for j in range(8):
@@ -33,6 +61,7 @@
             for i in range(j, 8):
                 e[j, i] = jnp.broadcast_to(c[i : i + 1, :], (8, BLK))
         r = [jnp.broadcast_to(rows[i : i + 1, :], (8, 256)) for i in range(8)]
+        cols = [[jnp.broadcast_to(n[:, 8 * g + j : 8 * g + j + 1], (8, BLK)) for j in range(8)] for n in ahead]
         out = None
         for j in range(8):
             s = rsqrt(e[j, j])
@@ -40,14 +69,20 @@
             for i in range(j + 1, 8):
                 for m in range(i, 8):
                     e[i, m] = e[i, m] - u[i] * u[m]
-            rj = r[j] * jnp.concatenate([s, s], axis=1)
+            rj = r[j] * wide(s)
             for i in range(j + 1, 8):
-                r[i] = r[i] - jnp.concatenate([u[i], u[i]], axis=1) * rj
+                r[i] = r[i] - wide(u[i]) * rj
+            for h in range(len(ahead)):
+                cj = cols[h][j] * s
+                for m in range(j + 1, 8):
+                    cols[h][m] = cols[h][m] - cj * u[m]
+                ahead[h] = ahead[h] - wide(cj) * rj
             out = rj if out is None else jnp.where(sub == j, rj, out)
         a_ref[8 * g : 8 * g + 8, :] = out
-        if g < 15:
-            t = tn(out[:, :BLK], out)
-            a_ref[8 * g + 8 :, :] = a_ref[8 * g + 8 :, :] - t[8 * g + 8 :, :]
+        low = 8 * (g + 1 + 2)
+        if low < BLK:
+            t = tn3(out[:, :BLK], out)
+            a_ref[low:, :] = a_ref[low:, :] - t[low:, :]
 
 def factor_steps(k_ref, l_ref, y_ref, a_ref, m_ref, progress):
     r_iota = lax.broadcasted_iota(jnp.int32, (BLK, BLK), 0)
@@ -78,7 +113,7 @@
 
         def update(i, c):
             rows = pl.ds(pl.multiple_of(i * BLK, BLK), BLK)
-            m_ref[rows, :] = m_ref[rows, :] - nt(l_ref[rows, at], l_ref[:, at])
+            m_ref[rows, :] = m_ref[rows, :] - nt3(l_ref[rows, at], l_ref[:, at])
             return c
 
         lax.fori_loop(b + 1, NPIV, update, 0)
@@ -440,70 +475,60 @@
     )(maps, where, buf)
 
 
-def split(x):
-    high = x.astype(jnp.bfloat16)
-    return high, (x - high.astype(jnp.float32)).astype(jnp.bfloat16)
-
-
-def dot3(a, b, dims):
-    def one(x, y):
-        return lax.dot_general(x, y, (dims, ((), ())), preferred_element_type=jnp.float32)
-
-    return one(a[0], b[0]) + (one(a[0], b[1]) + one(a[1], b[0]))
-
-
 NT = ((1,), (1,))
 NN = ((1,), (0,))
+
+
+def four(a, b, c, d):
+    return jnp.concatenate([jnp.concatenate([a, b], axis=1), jnp.concatenate([c, d], axis=1)], axis=0)
 
 
 def schur_kernel(
     where_ref, rows_ref, top_ref, moved_ref, front_ref, low_ref, inv_ref, out_ref,
     lh, ll, yh, yl, uh, ul, x_ref,
 ):
-    tile = pl.program_id(0)
     row, col, sub = where_ref[0], where_ref[1], where_ref[2]
-
-    @pl.when(tile == 0)
-    def _():
-        high, rest = split(low_ref[...])
-        lh[...] = high
-        ll[...] = rest
-        zero = jnp.zeros((BLK, BLK), jnp.float32)
-        for p in range(3):
-            first, second = inv_ref[2 * p], inv_ref[2 * p + 1]
-            at = 256 * p
-            cross = jnp.dot(low_ref[at + BLK : at + 256, at : at + BLK], first, precision=HI)
-            cross = -jnp.dot(second, cross, precision=HI)
-            pair = jnp.concatenate(
-                [jnp.concatenate([first, zero], axis=1), jnp.concatenate([cross, second], axis=1)], axis=0
-            )
-            high, rest = split(pair)
-            yh[p] = high
-            yl[p] = rest
+    high, rest = split(low_ref[...])
+    lh[...] = high
+    ll[...] = rest
+    zero = jnp.zeros((BLK, BLK), jnp.float32)
+    for p in range(3):
+        first, second = inv_ref[2 * p], inv_ref[2 * p + 1]
+        at = 256 * p
+        cross = jnp.dot(low_ref[at + BLK : at + 256, at : at + BLK], first, precision=HI)
+        cross = -jnp.dot(second, cross, precision=HI)
+        high, rest = split(four(first, zero, cross, second))
+        yh[p] = high
+        yl[p] = rest
+    for p in range(3):
+        at = 256 * p
+        x = four(top_ref[2 * p, 0], top_ref[2 * p, 1], top_ref[2 * p + 1, 0], top_ref[2 * p + 1, 1])
+        if p:
+            x = x - dot3((lh[at : at + 256, :at], ll[at : at + 256, :at]), (uh[:at, :], ul[:at, :]), NN)
+        high, rest = split(dot3((yh[p], yl[p]), split(x), NN))
+        uh[at : at + 256, :] = high
+        ul[at : at + 256, :] = rest
+
+    def tile(t):
+        here = pl.ds(pl.multiple_of(t * 256, 256), 256)
+        a, b = 2 * t, 2 * t + 1
+        acc = front_ref[here, :] + four(moved_ref[a, 0], moved_ref[a, 1], moved_ref[b, 0], moved_ref[b, 1])
+        xs = []
         for p in range(3):
             at = 256 * p
-            x = four(top_ref[2 * p, 0], top_ref[2 * p, 1], top_ref[2 * p + 1, 0], top_ref[2 * p + 1, 1])
-            if p:
-                x = x - dot3((lh[at : at + 256, :at], ll[at : at + 256, :at]), (uh[:at, :], ul[:at, :]), NN)
-            high, rest = split(dot3((yh[p], yl[p]), split(x), NN))
-            uh[at : at + 256, :] = high
-            ul[at : at + 256, :] = rest
-
-    acc = front_ref[...] + four(moved_ref[0, 0], moved_ref[0, 1], moved_ref[1, 0], moved_ref[1, 1])
-    xs = []
-    for p in range(3):
-        at = 256 * p
-        x = four(rows_ref[0, 2 * p], rows_ref[0, 2 * p + 1], rows_ref[1, 2 * p], rows_ref[1, 2 * p + 1])
-        for m in range(p):
-            cut = slice(256 * m, 256 * m + 256)
-            x = x - dot3(xs[m], (lh[at : at + 256, cut], ll[at : at + 256, cut]), NT)
-        x = dot3(split(x), (yh[p], yl[p]), NT)
-        x_ref[:, at : at + 256] = x
-        xs.append(split(x))
-        acc = acc - dot3(xs[p], (uh[at : at + 256, :], ul[at : at + 256, :]), NN)
-    out_ref[...] = acc
-
-    @pl.when((tile == 0) & (row < NPIV))
+            x = four(rows_ref[a, 2 * p], rows_ref[a, 2 * p + 1], rows_ref[b, 2 * p], rows_ref[b, 2 * p + 1])
+            for m in range(p):
+                cut = slice(256 * m, 256 * m + 256)
+                x = x - dot3(xs[m], (lh[at : at + 256, cut], ll[at : at + 256, cut]), NT)
+            x = dot3(split(x), (yh[p], yl[p]), NT)
+            x_ref[here, at : at + 256] = x
+            xs.append(split(x))
+            acc = acc - dot3(xs[p], (uh[at : at + 256, :], ul[at : at + 256, :]), NN)
+        out_ref[here, :] = acc
+
+    loop(0, 4, tile)
+
+    @pl.when(row < NPIV)
     def _():
         out_ref[:BLK, :] = jnp.zeros((BLK, 256), jnp.float32)
         x_ref[:BLK, :] = low_ref[pl.ds(pl.multiple_of(row * BLK, BLK), BLK), :]
@@ -513,26 +538,12 @@
         out_ref[:, :BLK] = x_ref[:, pl.ds(pl.multiple_of(col * BLK, BLK), BLK)]
 
 
-def four(a, b, c, d):
-    return jnp.concatenate([jnp.concatenate([a, b], axis=1), jnp.concatenate([c, d], axis=1)], axis=0)
-
-
 def schur(where, rows, top, moved, front, low, inv):
-    whole = lambda *shape: pl.BlockSpec(shape, lambda t: (0,) * len(shape), pipeline_mode=pl.Buffered(1))
     return pl.pallas_call(
         schur_kernel,
         out_shape=jax.ShapeDtypeStruct((1024, 256), jnp.float32),
-        grid=(4,),
-        in_specs=[
-            SM,
-            pl.BlockSpec((2, NPIV, BLK, BLK), lambda t: (t, 0, 0, 0)),
-            whole(NPIV, 2, BLK, BLK),
-            pl.BlockSpec((2, 2, BLK, BLK), lambda t: (t, 0, 0, 0)),
-            pl.BlockSpec((256, 256), lambda t: (t, 0)),
-            whole(PIV, PIV),
-            whole(NPIV, BLK, BLK),
-        ],
-        out_specs=pl.BlockSpec((256, 256), lambda t: (t, 0)),
+        in_specs=[SM] + [VM] * 6,
+        out_specs=VM,
         scratch_shapes=[
             pltpu.VMEM((PIV, PIV), jnp.bfloat16),
             pltpu.VMEM((PIV, PIV), jnp.bfloat16),
@@ -540,8 +551,9 @@
             pltpu.VMEM((3, 256, 256), jnp.bfloat16),
             pltpu.VMEM((PIV, 256), jnp.bfloat16),
             pltpu.VMEM((PIV, 256), jnp.bfloat16),
-            pltpu.VMEM((256, PIV), jnp.float32),
+            pltpu.VMEM((1024, PIV), jnp.float32),
         ],
+        compiler_params=pltpu.CompilerParams(vmem_limit_bytes=32 * 1024 * 1024),
         name="schur",
     )(where, rows, top, moved, front, low, inv)
 

time: 187 us -> 155 us (0.83)
  Pallas kernels: 173 us -> 145 us
  local copies, waits for them, and re-layouts: 12.2 us -> 6.5 us
    pallas_call x1, Pallas kernels: 92.2 us -> 67.6 us  [factor_all(): pl.pallas_call(factor_kernel, out_shape=(f32(PIV, PIV), f32(NPIV, BLK, BL...]
    unnamed x16 -> x10, local copies, waits for them, and re-layouts: 6.94 us -> 1.24 us
where the time goes in v5:
time: 155 us
  Pallas kernels  145 us (94%)
  local copies, waits for them, and re-layouts  6.5 us (4%)
  other arithmetic  2.87 us (2%)
    pallas_call x1, Pallas kernels, factor_all(): pl.pallas_call(factor_kernel, out_shape=(f32(PIV, PIV), f32(NPIV, BLK, BL...  67.6 us
    pallas_call x1, Pallas kernels, gather_all(): pl.pallas_call(gather_kernel, out_shape=(jax.ShapeDtypeStruct((NTILE, 32,...  59.8 us
    pallas_call x1, Pallas kernels, schur(): pl.pallas_call(schur_kernel, out_shape=jax.ShapeDtypeStruct((1024, 256),...  11.9 us
    pallas_call x1, Pallas kernels, place(): pl.pallas_call(place_kernel, out_shape=jax.ShapeDtypeStruct((32, 8, 2, 4,...  5.74 us

profile of v5, /device:TPU:2, one launch (start us, length us, event | category | flops | bytes accessed | tf_op | source)
XLA Modules:
  0.0 154.5 jit_solution(1732685563703408802)
XLA Ops:
  0.0 0.6 pad_add_fusion.where_ref
  0.6 0.7 convert_bitcast_fusion
  1.3 0.7 broadcast_in_dim.2.map_ref
  1.9 0.9 copy_bitcast_fusion
  2.9 1.1 reshape_squeeze.3
  3.9 0.7 copy.6
  4.7 1.9 %slice.9 = f32[1024,128]{1,0:T(8,128)} slice(f32[1024,256]{1,0:T(8,128)} %front_ref.1), slice={[0:1024], [0:128]} | slice | bytes 1048576 | tf_op jit(solution)/shard_map/slice | solution.py:565
  6.5 59.8 %gather_all.1 = (f32[21,32,4,128]{3,2,1,0:T(4,128)}, f32[4,16,128]{2,1,0:T(8,128)}, f32[8,32,2,2,4,128]{5,4,3,2,1,0:T(4,128)}, f32[6,8,4,128]{3,2,1,0:T(4,128)}) custom-call(f32[2,2,32,4,128]{4,3,2,1,0:T(4,128)} %bitcast.27, f32[8,32,4,128]{3,2,1,0:T(4,128)} %bitcast.26, f32[16,128]{1,0:T(8,128)} %broadcast_in_dim.2.map_ref), custom_call_target="tpu_custom_call" | custom-call | tf_op jit(solution)/shard_map/gather_all/pallas_call | solution.py:333
  66.4 0.0 copy-start.2
  66.4 0.0 copy-start.3
  66.4 1.6 %convert_reduce_fusion.map_ref = s32[4,16]{1,0:T(4,128)} fusion(f32[4,16,128]{2,1,0:T(8,128)} %get-tuple-element.15), kind=kLoop, calls=%fused_computation.2 | loop fusion | flops 64 | bytes 512 | tf_op jit(solution)/shard_map/convert_element_type | solution.py:566
  68.0 0.0 copy-start.1
  68.0 0.0 copy-start.4
  68.0 5.7 %place.1.acc_ref = f32[32,8,2,4,128]{4,3,2,1,0:T(4,128)} custom-call(s32[4,16]{1,0:T(4,128)} %convert_reduce_fusion.map_ref, s32[3]{0:T(128)} %pad_add_fusion.where_ref, f32[8,32,2,2,4,128]{5,4,3,2,1,0:T(4,128)} %get-tuple-element.16.buf_ref), custom_call_target="tpu_custom_call" | custom-call | tf_op jit(solution)/shard_map/place/pallas_call | solution.py:469
  73.7 0.0 copy-done.2
  73.7 0.0 copy-done.3
  73.8 0.0 copy-start
  73.8 1.2 copy-done
  75.0 67.6 %factor_all.1 = (f32[768,768]{1,0:T(8,128)S(1)}, f32[6,128,128]{2,1,0:T(8,128)S(1)}, f32[8,6,32,4,128]{4,3,2,1,0:T(4,128)S(1)}, f32[8,2,32,4,128]{4,3,2,1,0:T(4,128)S(1)}, f32[6,2,32,4,128]{4,3,2,1,0:T(4,128)S(1)}) custom-call(f32[21,128,128]{2,1,0:T(8,128)S(1)} %bitcast.22, f32[32,8,2,4,128]{4,3,2,1,0:T(4,128)S(1)} %copy-done, ...), custom_call_target="tpu_custom_call" | custom-call | tf_op jit(solution)/shard_map/factor_all/pallas_call | solution.py:425
  142.6 0.0 copy-done.1
  142.6 0.0 copy-done.4
  142.6 11.9 %schur.1 = f32[1024,256]{1,0:T(8,128)} custom-call(s32[3]{0:T(128)S(1)} %copy-done.4, f32[8,6,128,128]{3,2,1,0:T(8,128)S(1)} %bitcast.21, f32[6,2,128,128]{3,2,1,0:T(8,128)S(1)} %bitcast.24, f32[8,2,128,128]{3,2,1,0:T(8,128)S(1)} %bitcast.23, f32[1024,256]{1,0:T(8,128)S(1)} %copy-done.1, f32[768,768]{1,0:T(8,128)S(1)} %get-tuple-element.21.low_ref, ...), custom_call_target="tpu_custom_call" | custom-call | tf_op jit(solution)/shard_map/schur/pallas_call | solution.py:542
Async XLA Ops:
  66.4 7.4 %copy-start.2 = (f32[21,32,4,128]{3,2,1,0:T(4,128)S(1)}, f32[21,32,4,128]{3,2,1,0:T(4,128)}, u32[]{:S(2)}) copy-start(f32[21,32,4,128]{3,2,1,0:T(4,128)} %get-tuple-element.14) | copy-start | bytes 4128772
  66.4 7.4 %copy-start.3 = (f32[6,8,4,128]{3,2,1,0:T(4,128)S(1)}, f32[6,8,4,128]{3,2,1,0:T(4,128)}, u32[]{:S(2)}) copy-start(f32[6,8,4,128]{3,2,1,0:T(4,128)} %get-tuple-element.17.panel_ref) | copy-start | bytes 294916
  68.0 74.6 %copy-start.1 = (f32[1024,256]{1,0:T(8,128)S(1)}, f32[1024,256]{1,0:T(8,128)}, u32[]{:S(2)}) copy-start(f32[1024,256]{1,0:T(8,128)} %front_ref.1) | copy-start | bytes 3145732
  68.0 74.6 %copy-start.4 = (s32[3]{0:T(128)S(1)}, s32[3]{0:T(128)}, u32[]{:S(2)}) copy-start(s32[3]{0:T(128)} %pad_add_fusion.where_ref) | copy-start | bytes 40
  73.8 1.2 copy-start

commit v6 on v5

--- a/solution.py
+++ b/solution.py
@@ -183,14 +183,12 @@
 
 def gather_kernel(
     child_ref, front_ref, map_ref, k_ref, maps_ref, buf_ref, panel_ref,
-    z_ref, acc_ref, send, got, z_got, f_got, k_got, p_got, right_got, left_got,
+    z_ref, acc_ref, send, got, z_got, f_got, k_got, p_got, ring_got,
 ):
     at = Place()
     r, c, s, e = at.r, at.c, at.s, at.e
     at.greet()
-    pivot_row = r < NPIV
     has_front = (c < NPIV) & (s == 0)
-    spot = jnp.minimum(r, NPIV - 1)
     seat = jnp.minimum(c, NPIV - 1)
 
     def child_copy(d):
@@ -199,7 +197,11 @@
 
     def front_copy(d):
         p, device = at.plane(d)
-        return push(front_ref.at[:, p], panel_ref.at[seat], send.at[1], got.at[1], device)
+        return push(front_ref.at[0, p], panel_ref.at[seat, 0], send.at[1], got.at[1], device)
+
+    def rest_copy(d):
+        p, device = at.plane(d)
+        return push(front_ref.at[pl.ds(1, 7), p], panel_ref.at[seat, pl.ds(1, 7)], send.at[4], got.at[4], device)
 
     def map_copy(d):
         return push(map_ref, maps_ref.at[s], send.at[2], got.at[2], (r, c, (s + d) % 4))
@@ -210,49 +212,63 @@
 
     @pl.when(has_front)
     def _():
-        pltpu.make_async_copy(front_ref.at[:, e], panel_ref.at[seat], got.at[1]).start()
+        pltpu.make_async_copy(front_ref.at[0, e], panel_ref.at[seat, 0], got.at[1]).start()
         loop(1, 32, lambda d: front_copy(d).start())
 
     for d in range(1, 4):
         map_copy(d).start()
 
-    def z_copy(d):
-        return push(buf_ref.at[spot, pl.ds(0, 24), 0, 0], z_ref.at[spot, pl.ds(0, 24)], send.at[3], z_got.at[spot], at.line(d))
-
-    def f_copy(d):
-        return push(panel_ref.at[:, 0], z_ref.at[spot, pl.ds(24, 6)], send.at[4], f_got.at[spot], at.line(d))
-
-    def right_copy(k):
-        block = (r + 8 - k) % 8
-        return push(buf_ref.at[block], buf_ref.at[block], send.at[5], right_got.at[k], at.line(1))
-
-    def left_copy(k):
-        block = (r + k) % 8
-        return push(buf_ref.at[block], buf_ref.at[block], send.at[6], left_got.at[k], at.line(7))
-
-    def right_wait(k):
-        arrive(buf_ref.at[(r + 7 - k) % 8], right_got.at[k])
-
-    def left_wait(k):
-        arrive(buf_ref.at[(r + 1 + k) % 8], left_got.at[k])
+    def z_copies(i, d):
+        device = at.line(d)
+        tiles, own = pl.ds(0, 4 * (i + 1)), pl.ds(0, i + 1)
+        return (
+            push(buf_ref.at[i, tiles, 0, 0], z_ref.at[i, tiles], send.at[3], z_got.at[i], device),
+            push(panel_ref.at[own, 0], z_ref.at[i, pl.ds(24, i + 1)], send.at[3], f_got.at[i], device),
+        )
+
+    def ring_copy(way, k, h):
+        block = (r + 8 - k) % 8 if way == 0 else (r + k) % 8
+        half = buf_ref.at[block, :, h]
+        return push(half, half, send.at[5 + way], ring_got.at[way, 2 * k + h], at.line(1 if way == 0 else 7))
+
+    def ring_wait(way, k, h):
+        block = (r + 7 - k) % 8 if way == 0 else (r + 1 + k) % 8
+        arrive(buf_ref.at[block, :, h], ring_got.at[way, 2 * k + h])
+
+    hops = [(way, k, h) for k in range(4) for h in range(2) for way in range(2) if k < 3 or h == way]
+
+    def ring_step(k):
+        for hop in hops:
+            if hop[1] == k:
+                if k:
+                    ring_wait(hop[0], k - 1, hop[2])
+                ring_copy(*hop).start()
 
     arrive(buf_ref.at[r], got.at[0])
-    arrive(panel_ref, got.at[1])
-
-    @pl.when(pivot_row)
+    arrive(panel_ref.at[:, 0], got.at[1])
+
+    for i in range(NPIV):
+        @pl.when(r == i)
+        def _():
+            tiles, own = pl.ds(0, 4 * (i + 1)), pl.ds(0, i + 1)
+            pltpu.make_async_copy(buf_ref.at[i, tiles, 0, 0], z_ref.at[i, tiles], z_got.at[i]).start()
+            pltpu.make_async_copy(panel_ref.at[own, 0], z_ref.at[i, pl.ds(24, i + 1)], f_got.at[i]).start()
+            for d in (4, 3, 5, 2, 6, 1, 7):
+                for copy in z_copies(i, d):
+                    copy.start()
+
+    @pl.when(has_front)
     def _():
-        pltpu.make_async_copy(buf_ref.at[spot, pl.ds(0, 24), 0, 0], z_ref.at[spot, pl.ds(0, 24)], z_got.at[spot]).start()
-        pltpu.make_async_copy(panel_ref.at[:, 0], z_ref.at[spot, pl.ds(24, 6)], f_got.at[spot]).start()
-        for d in (4, 3, 5, 2, 6, 1, 7):
-            z_copy(d).start()
-            f_copy(d).start()
-
-    right_copy(0).start()
-    left_copy(0).start()
+        pltpu.make_async_copy(front_ref.at[pl.ds(1, 7), e], panel_ref.at[seat, pl.ds(1, 7)], got.at[4]).start()
+        loop(1, 32, lambda d: rest_copy(d).start())
+
+    ring_step(0)
+    for i in range(NPIV - 1):
+        z_ref[i, 4 * (i + 1) : 24] = jnp.zeros((20 - 4 * i, 4, BLK), jnp.float32)
     arrive(maps_ref, got.at[2])
     for i in range(NPIV):
-        arrive(z_ref.at[i, pl.ds(0, 24)], z_got.at[i])
-        arrive(z_ref.at[i, pl.ds(24, 6)], f_got.at[i])
+        arrive(z_ref.at[i, pl.ds(0, 4 * (i + 1))], z_got.at[i])
+        arrive(z_ref.at[i, pl.ds(24, i + 1)], f_got.at[i])
 
     for t, (i, j) in enumerate(TILES):
         acc_ref[t] = z_ref[i, 24 + j]
@@ -263,13 +279,13 @@
         for j in range(NPIV):
             strip = None
             for seat_j in range(j + 1):
-                pick = jnp.where(wanted[seat_j : seat_j + 1] == float(j), 1.0, 0.0)[None]
+                pick = jnp.where(wanted[seat_j : seat_j + 1] == j, 1.0, 0.0)[None]
                 term = z_ref[:, seat_j * 4 + q] * pick
                 strip = term if strip is None else strip + term
             strips.append(strip)
         for j in range(NPIV):
             for i in range(j, NPIV):
-                pick = jnp.where(wanted == float(i), 1.0, 0.0)[:, None, :]
+                pick = jnp.where(wanted == i, 1.0, 0.0)[:, None, :]
                 acc_ref[i * (i + 1) // 2 + j] += jnp.sum(strips[j] * pick, axis=0)
 
     loop(0, 4, add_child)
@@ -289,22 +305,18 @@
         pair_copy(d).start()
 
     loop(1, 16, lambda d: k_copy(d).start())
-    right_wait(0)
-    right_copy(1).start()
-    left_wait(0)
-    left_copy(1).start()
+    ring_step(1)
     own_k.wait()
     pair_copy(0).start()
-    right_wait(1)
-    right_copy(2).start()
-    left_wait(1)
-    left_copy(2).start()
+    ring_step(2)
     loop(1, 16, forward)
-    right_wait(2)
-    right_copy(3).start()
-    left_wait(2)
+    ring_step(3)
     loop(0, 16, lambda d: pair_copy(d).wait())
-    right_wait(3)
+    arrive(panel_ref.at[:, pl.ds(1, 7)], got.at[4])
+    ring_wait(0, 2, 1)
+    ring_wait(1, 2, 0)
+    ring_wait(0, 3, 0)
+    ring_wait(1, 3, 1)
 
     loop(1, 16, lambda d: k_copy(d).wait_send())
     loop(1, 32, lambda d: child_copy(d).wait_send())
@@ -312,20 +324,19 @@
     @pl.when(has_front)
     def _():
         loop(1, 32, lambda d: front_copy(d).wait_send())
+        loop(1, 32, lambda d: rest_copy(d).wait_send())
 
     for d in range(1, 4):
         map_copy(d).wait_send()
-
-    @pl.when(pivot_row)
-    def _():
-        for d in range(1, 8):
-            z_copy(d).wait_send()
-            f_copy(d).wait_send()
-
-    for k in range(4):
-        right_copy(k).wait_send()
-    for k in range(3):
-        left_copy(k).wait_send()
+    for i in range(NPIV):
+        @pl.when(r == i)
+        def _():
+            for d in range(1, 8):
+                for copy in z_copies(i, d):
+                    copy.wait_send()
+
+    for hop in hops:
+        ring_copy(*hop).wait_send()
 
 
 def gather_all(child, front, child_map):
@@ -334,7 +345,7 @@
         gather_kernel,
         out_shape=(
             jax.ShapeDtypeStruct((NTILE, 32, 4, BLK), jnp.float32),
-            jax.ShapeDtypeStruct((4, 16, BLK), jnp.float32),
+            jax.ShapeDtypeStruct((4, 16, BLK), jnp.int32),
             jax.ShapeDtypeStruct((8, 32, 2, 2, 4, BLK), jnp.float32),
             jax.ShapeDtypeStruct((NPIV, 8, 4, BLK), jnp.float32),
         ),
@@ -343,7 +354,7 @@
         scratch_shapes=[
             pltpu.VMEM((NPIV, 30, 4, BLK), jnp.float32),
             pltpu.VMEM((NTILE, 4, BLK), jnp.float32),
-            dma((9,)), dma((4,)), dma((NPIV,)), dma((NPIV,)), dma((16,)), dma((16,)), dma((4,)), dma((3,)),
+            dma((9,)), dma((5,)), dma((NPIV,)), dma((NPIV,)), dma((16,)), dma((16,)), dma((2, 8)),
         ],
         compiler_params=pltpu.CompilerParams(collective_id=0, has_side_effects=True),
         name="gather_all",
@@ -402,8 +413,8 @@
         pair_copy(d).start()
 
     def progress(b):
-        pl.when(b == 1)(after_first)
-        pl.when(b == 3)(lambda: loop(1, 16, forward))
+        pl.when(b == 2)(after_first)
+        pl.when(b == 4)(lambda: loop(1, 16, forward))
 
     factor_steps(k_ref, low_ref, inv_ref, a_ref, m_ref, progress)
 
@@ -445,34 +456,34 @@
     )(k, acc, panel, front)
 
 
-def place_kernel(map_ref, where_ref, buf_ref, acc_ref):
+def place_kernel(map_ref, buf_ref, acc_ref):
     acc_ref[...] = jnp.zeros_like(acc_ref)
-    row = where_ref[0]
+    row = lax.axis_index("row")
 
     def child_row(step):
         q = step // 16
         block_row = step % 16
-        i = map_ref[q, block_row]
+        i = map_ref[q, block_row, 0]
 
         @pl.when(i % 8 == row)
         def _():
             slot = i // 8
             for block_col in range(16):
-                j = map_ref[q, block_col]
+                j = map_ref[q, block_col, 0]
                 tile = buf_ref[block_row % 8, block_col % 8 * 4 + q, block_row // 8, block_col // 8]
                 acc_ref[j % 8 * 4 + j // 16, slot, (j // 8) % 2] += tile
 
     loop(0, 64, child_row)
 
 
-def place(maps, where, buf):
+def place(maps, buf):
     return pl.pallas_call(
         place_kernel,
         out_shape=jax.ShapeDtypeStruct((32, 8, 2, 4, BLK), jnp.float32),
-        in_specs=[SM, SM, VM],
+        in_specs=[SM, VM],
         out_specs=VM,
         name="place",
-    )(maps, where, buf)
+    )(maps, buf)
 
 
 NT = ((1,), (1,))
@@ -484,10 +495,10 @@
 
 
 def schur_kernel(
-    where_ref, rows_ref, top_ref, moved_ref, front_ref, low_ref, inv_ref, out_ref,
+    rows_ref, top_ref, moved_ref, front_ref, low_ref, inv_ref, out_ref,
     lh, ll, yh, yl, uh, ul, x_ref,
 ):
-    row, col, sub = where_ref[0], where_ref[1], where_ref[2]
+    row, col, sub = (lax.axis_index(a) for a in ("row", "col", "sub"))
     high, rest = split(low_ref[...])
     lh[...] = high
     ll[...] = rest
@@ -538,11 +549,11 @@
         out_ref[:, :BLK] = x_ref[:, pl.ds(pl.multiple_of(col * BLK, BLK), BLK)]
 
 
-def schur(where, rows, top, moved, front, low, inv):
+def schur(rows, top, moved, front, low, inv):
     return pl.pallas_call(
         schur_kernel,
         out_shape=jax.ShapeDtypeStruct((1024, 256), jnp.float32),
-        in_specs=[SM] + [VM] * 6,
+        in_specs=[VM] * 6,
         out_specs=VM,
         scratch_shapes=[
             pltpu.VMEM((PIV, PIV), jnp.bfloat16),
@@ -555,19 +566,17 @@
         ],
         compiler_params=pltpu.CompilerParams(vmem_limit_bytes=32 * 1024 * 1024),
         name="schur",
-    )(where, rows, top, moved, front, low, inv)
+    )(rows, top, moved, front, low, inv)
 
 
 def body(front, child, child_map):
-    where = jnp.stack([lax.axis_index(a) for a in ("row", "col", "sub")]).astype(jnp.int32)
-    wide = jnp.broadcast_to(child_map[0].astype(jnp.float32)[:, None], (16, BLK))
+    wide = jnp.broadcast_to(child_map[0][:, None], (16, BLK))
     shares = child[0].reshape(2, BLK, 2, BLK).transpose(0, 2, 1, 3).reshape(2, 2, 32, 4, BLK)
     k, maps, buf, panel = gather_all(shares, front[:, :BLK].reshape(8, 32, 4, BLK), wide)
-    acc = place(maps[:, :, 0].astype(jnp.int32), where, buf)
+    acc = place(maps, buf)
     first = front[:BLK].reshape(BLK, 2, BLK).transpose(1, 0, 2).reshape(2, 32, 4, BLK)
     low, inv, rows, moved, top = factor_all(k.reshape(NTILE, BLK, BLK), acc, panel, first)
     return schur(
-        where,
         rows.reshape(8, NPIV, BLK, BLK),
         top.reshape(NPIV, 2, BLK, BLK),
         moved.reshape(8, 2, BLK, BLK),

time: 155 us -> 132 us (0.85)
  Pallas kernels: 145 us -> 123 us
  other arithmetic: 2.87 us -> 0 us
    pallas_call x1, Pallas kernels: 59.8 us -> 48.6 us  [gather_all(): pl.pallas_call(gather_kernel, out_shape=(jax.ShapeDtypeStruct((NTILE, 32,...]
    pallas_call x1, Pallas kernels: 67.6 us -> 56.4 us  [factor_all(): pl.pallas_call(factor_kernel, out_shape=(f32(PIV, PIV), f32(NPIV, BLK, BL...]
    convert_element_type x2 -> x0, other arithmetic: 2.26 us -> none  [the longest x1 1.61 us: body(): acc = place(maps[:, :, 0].astype(jnp.int32), where, buf)]
where the time goes in v6:
time: 132 us; the launch traced here: 130 us
  Pallas kernels  123 us (93%)
  local copies, waits for them, and re-layouts  7.13 us (5%)
    pallas_call x1, Pallas kernels, factor_all(): pl.pallas_call(factor_kernel, out_shape=(f32(PIV, PIV), f32(NPIV, BLK, BL...  56.4 us
    pallas_call x1, Pallas kernels, gather_all(): pl.pallas_call(gather_kernel, out_shape=(jax.ShapeDtypeStruct((NTILE, 32,...  48.6 us
    pallas_call x1, Pallas kernels, schur(): pl.pallas_call(schur_kernel, out_shape=jax.ShapeDtypeStruct((1024, 256),...  11.4 us
    pallas_call x1, Pallas kernels, place(): pl.pallas_call(place_kernel, out_shape=jax.ShapeDtypeStruct((32, 8, 2, 4,...  6.42 us

profile of v6, /device:TPU:2, one launch (start us, length us, event | category | flops | bytes accessed | tf_op | source)
XLA Modules:
  0.0 130.0 jit_solution(15288617588036949003)
XLA Ops:
  0.0 1.3 %broadcast_in_dim.8.map_ref = s32[16,128]{1,0:T(8,128)} broadcast(s32[16]{0:T(128)} %bitcast.24), dimensions={0} | broadcast | bytes 8256 | tf_op jit(solution)/shard_map/broadcast_in_dim | solution.py:573
  1.3 0.9 copy_bitcast_fusion
  2.2 1.1 reshape_squeeze.3
  3.3 0.7 copy.4
  4.0 1.9 %slice.6 = f32[1024,128]{1,0:T(8,128)} slice(f32[1024,256]{1,0:T(8,128)} %front_ref.1), slice={[0:1024], [0:128]} | slice | bytes 1048576 | tf_op jit(solution)/shard_map/slice | solution.py:575
  5.9 48.6 %gather_all.1 = (f32[21,32,4,128]{3,2,1,0:T(4,128)}, s32[4,16,128]{2,1,0:T(8,128)}, f32[8,32,2,2,4,128]{5,4,3,2,1,0:T(4,128)}, f32[6,8,4,128]{3,2,1,0:T(4,128)}) custom-call(f32[2,2,32,4,128]{4,3,2,1,0:T(4,128)} %bitcast.23, f32[8,32,4,128]{3,2,1,0:T(4,128)} %bitcast.22, s32[16,128]{1,0:T(8,128)} %broadcast_in_dim.8.map_ref), custom_call_target="tpu_custom_call" | custom-call | tf_op jit(solution)/shard_map/gather_all/pallas_call | solution.py:344
  54.5 0.0 copy-start.2
  54.5 0.0 copy-start.3
  54.5 0.0 copy-start.1
  54.6 6.4 %place.1.acc_ref = f32[32,8,2,4,128]{4,3,2,1,0:T(4,128)} custom-call(s32[4,16,128]{2,1,0:T(8,128)} %get-tuple-element.15.map_ref, f32[8,32,2,2,4,128]{5,4,3,2,1,0:T(4,128)} %get-tuple-element.16.buf_ref), custom_call_target="tpu_custom_call" | custom-call | tf_op jit(solution)/shard_map/place/pallas_call | solution.py:480
  61.0 0.0 copy-done.2
  61.0 0.0 copy-done.3
  61.0 0.0 copy-start
  61.0 1.2 copy-done
  62.2 56.4 %factor_all.1 = (f32[768,768]{1,0:T(8,128)S(1)}, f32[6,128,128]{2,1,0:T(8,128)S(1)}, f32[8,6,32,4,128]{4,3,2,1,0:T(4,128)S(1)}, f32[8,2,32,4,128]{4,3,2,1,0:T(4,128)S(1)}, f32[6,2,32,4,128]{4,3,2,1,0:T(4,128)S(1)}) custom-call(f32[21,128,128]{2,1,0:T(8,128)S(1)} %bitcast.18, f32[32,8,2,4,128]{4,3,2,1,0:T(4,128)S(1)} %copy-done, ...), custom_call_target="tpu_custom_call" | custom-call | tf_op jit(solution)/shard_map/factor_all/pallas_call | solution.py:436
  118.6 0.0 copy-done.1
  118.6 11.4 %schur.1 = f32[1024,256]{1,0:T(8,128)} custom-call(f32[8,6,128,128]{3,2,1,0:T(8,128)S(1)} %bitcast.17, f32[6,2,128,128]{3,2,1,0:T(8,128)S(1)} %bitcast.20, f32[8,2,128,128]{3,2,1,0:T(8,128)S(1)} %bitcast.19, f32[1024,256]{1,0:T(8,128)S(1)} %copy-done.1, f32[768,768]{1,0:T(8,128)S(1)} %get-tuple-element.21.low_ref, f32[6,128,128]{2,1,0:T(8,128)S(1)} %get-tuple-element.22.inv_ref), custom_call_target="tpu_custom_call" | custom-call | tf_op jit(solution)/shard_map/schur/pallas_call | solution.py:553
Async XLA Ops:
  54.5 6.5 %copy-start.2 = (f32[21,32,4,128]{3,2,1,0:T(4,128)S(1)}, f32[21,32,4,128]{3,2,1,0:T(4,128)}, u32[]{:S(2)}) copy-start(f32[21,32,4,128]{3,2,1,0:T(4,128)} %get-tuple-element.14) | copy-start | bytes 4128772
  54.5 6.4 %copy-start.3 = (f32[6,8,4,128]{3,2,1,0:T(4,128)S(1)}, f32[6,8,4,128]{3,2,1,0:T(4,128)}, u32[]{:S(2)}) copy-start(f32[6,8,4,128]{3,2,1,0:T(4,128)} %get-tuple-element.17.panel_ref) | copy-start | bytes 294916
  54.5 64.1 %copy-start.1 = (f32[1024,256]{1,0:T(8,128)S(1)}, f32[1024,256]{1,0:T(8,128)}, u32[]{:S(2)}) copy-start(f32[1024,256]{1,0:T(8,128)} %front_ref.1) | copy-start | bytes 3145732
  61.0 1.2 copy-start
